TPU v7x, 128 devices: a whole 4x4x4 slice. The times are simulated.
128 devices in a mesh: seq: 32 (over z, x, core), dp: 4 (over y).
Axes of the slice: x: 4, y: 4, z: 4, core: 2. Of those that a mesh axis runs over, the one named last changes fastest.
Arguments:
- queries: bfloat16 [4, 8192, 1024], P('dp', 'seq'), may hold values from -8 to 8
- key_rows: bfloat16 [4, 8192, 1024], P('dp', 'seq'), may hold values from -8 to 8
- value_rows: bfloat16 [4, 8192, 1024], P('dp', 'seq'), may hold values from -16 to 16
- conv_key: float32 [5, 4, 1024], replicated, may hold values from -2.5 to 2.5
- conv_value: float32 [5, 4, 1024], replicated, may hold values from -2.5 to 2.5
- grad_out: bfloat16 [4, 8192, 1024], P('dp', 'seq'), may hold values from -12 to 12
Outputs:
- attended: bfloat16 [4, 8192, 1024], P('dp', 'seq')
- grad_query: bfloat16 [4, 8192, 1024], P('dp', 'seq')
- grad_key: bfloat16 [4, 8192, 1024], P('dp', 'seq')
- grad_value: bfloat16 [4, 8192, 1024], P('dp', 'seq')
- grad_conv_key: float32 [5, 4, 1024], replicated
- grad_conv_value: float32 [5, 4, 1024], replicated
All inputs are finite; a program needn't handle non-finite values.
Results may differ from a plain program's by a relative error of at most 0.019.
Values may be sent and summed in bfloat16 or wider, within the bound.
No kernel may reach another device: no remote copies, remote signals or barrier semaphores. Data moves between devices by JAX's collectives and lax.ppermute only.
A program may use at most 128 MiB of HBM per device.

v0:
```python
import jax
import jax.numpy as jnp
from jax import lax
from jax.sharding import PartitionSpec as P

HEADS = 8
HEAD_DIM = 128
BLOCK = 128


def passed_along(value, axis, steps):
    count = lax.axis_size(axis)
    initial, last = (max(0, -steps), min(count, count - steps))
    return lax.ppermute(value, axis, [(source, source + steps) for source in range(initial, last)])


def partner_2(array, axis, distance):
    return lax.ppermute(array, axis, [(i, i ^ 1 << distance) for i in range(lax.axis_size(axis))])


def coarsen(extended, weight):
    out_rows = (extended.shape[1] - 2) // 2
    summed = weight[0] * extended[:, 0 : 2 * out_rows : 2].astype(jnp.float32)
    for offset in range(1, 4):
        summed = summed + weight[offset] * extended[:, offset : offset + 2 * out_rows : 2].astype(
            jnp.float32
        )
    return summed.astype(jnp.bfloat16)


def coarsen_back(upstream, extended, weight):
    seqs_dev, out_rows, feat_width = upstream.shape
    zero_row = jnp.zeros((seqs_dev, 1, feat_width), jnp.float32)
    even_rows = jnp.concatenate([weight[0] * upstream, zero_row], 1) + jnp.concatenate(
        [zero_row, weight[2] * upstream], 1
    )
    odd_rows = jnp.concatenate([weight[1] * upstream, zero_row], 1) + jnp.concatenate(
        [zero_row, weight[3] * upstream], 1
    )
    spread = jnp.stack([even_rows, odd_rows], 2).reshape(seqs_dev, 2 * out_rows + 2, feat_width)
    weight_grad = jnp.stack(
        [
            jnp.sum(
                upstream * extended[:, offset : offset + 2 * out_rows : 2].astype(jnp.float32),
                (0, 1),
            )
            for offset in range(4)
        ]
    )
    return (spread, weight_grad)


def move_near(moved_rows, shift_by):
    return passed_along(moved_rows, "seq", shift_by)


def move_grads(moved_rows, shift_by):
    return passed_along(moved_rows.astype(jnp.bfloat16), "seq", shift_by).astype(moved_rows.dtype)


def per_device(queries, key_rows, value_rows, conv_key, conv_value, grad_out):
    seqs_dev, tok_rows, feat_width = queries.shape
    levels = conv_key.shape[0]
    head_count = HEADS
    head_size = HEAD_DIM
    blk_rows = BLOCK
    blocks_here = tok_rows // blk_rows
    local_top = blocks_here.bit_length() - 1
    seq_devices = lax.axis_size("seq")
    dev_index = lax.axis_index("seq")
    total_blocks = blocks_here * seq_devices
    score_scale = head_size ** (-0.5)
    pair_width = 2 * feat_width
    group_heads = 2
    kv_weight = jnp.stack(
        [
            conv_key.reshape(levels, 4, head_count, head_size),
            conv_value.reshape(levels, 4, head_count, head_size),
        ],
        3,
    ).reshape(levels, 4, pair_width)
    fine_pairs = jnp.stack(
        [
            key_rows.reshape(seqs_dev, tok_rows, head_count, head_size),
            value_rows.reshape(seqs_dev, tok_rows, head_count, head_size),
        ],
        3,
    ).reshape(seqs_dev, tok_rows, pair_width)
    own_rows = [fine_pairs]
    left_rims = [move_near(fine_pairs[:, -blk_rows:], 1)]
    right_rims = [move_near(fine_pairs[:, :blk_rows], -1)]
    extended_local = [None]
    level_id = 1
    extended = jnp.concatenate([left_rims[level_id - 1][:, -2:], own_rows[level_id - 1]], 1)
    extended_local.append(extended)
    coarse = coarsen(extended, kv_weight[level_id - 1])
    own_rows.append(coarse)
    left_rims.append(move_near(coarse, 1))
    right_rims.append(move_near(coarse, -1))
    block_now = own_rows[local_top]
    left_now = left_rims[local_top]
    group_lefts, group_rights, group_extended, group_first = ([], [], [], [])
    for level_id in range(local_top + 1, levels + 1):
        swap_bit = level_id - local_top - 1
        extended = jnp.concatenate([left_now[:, -2:], block_now], 1)
        group_extended.append(extended)
        own_half = coarsen(extended, kv_weight[level_id - 1])
        partner = partner_2(own_half, "seq", swap_bit)
        is_first = dev_index // 2**swap_bit % 2 == 0
        group_first.append(is_first)
        block_now = jnp.where(
            is_first,
            jnp.concatenate([own_half, partner], 1),
            jnp.concatenate([partner, own_half], 1),
        )
        stride_dev = 2 ** (level_id - local_top)
        left_now = move_near(block_now, stride_dev)
        right_now = move_near(block_now, -stride_dev)
        group_lefts.append(left_now)
        group_rights.append(right_now)
    glob_blocks = dev_index * blocks_here + jnp.arange(blocks_here, dtype=jnp.int32)
    always = jnp.ones((blocks_here,), jnp.bool_)
    sources = []
    pieces = []
    for level_id in range(local_top + 1):
        block_count = blocks_here >> level_id
        padded = jnp.concatenate([left_rims[level_id], own_rows[level_id], right_rims[level_id]], 1)
        sources.append(
            padded.reshape(seqs_dev, block_count + 2, blk_rows, head_count, 2, head_size)
        )
        coarse_id = glob_blocks // 2**level_id
        spread = 2**level_id
        pieces.append((level_id, 0, spread, coarse_id >= 1))
        if level_id == 0:
            pieces.append((0, 1, 1, always))
        pieces.append((level_id, 2, spread, coarse_id + 1 < total_blocks // 2**level_id))
    for slot_id in range(levels - local_top):
        level_id = local_top + 1 + slot_id
        coarse_id = glob_blocks // 2**level_id
        sources.append(
            group_lefts[slot_id].reshape(seqs_dev, 1, blk_rows, head_count, 2, head_size)
        )
        pieces.append((len(sources) - 1, 0, blocks_here, coarse_id >= 1))
        sources.append(
            group_rights[slot_id].reshape(seqs_dev, 1, blk_rows, head_count, 2, head_size)
        )
        pieces.append(
            (len(sources) - 1, 0, blocks_here, coarse_id + 1 < total_blocks // 2**level_id)
        )
    query_blocks = queries.reshape(seqs_dev, blocks_here, blk_rows, head_count, head_size)
    out_blocks = grad_out.reshape(seqs_dev, blocks_here, blk_rows, head_count, head_size)

    def head_group(group_id, loop_state):
        attended_acc, grad_q_acc, source_grads, log_totals, row_deltas = loop_state
        head_start = group_id * group_heads
        q_part = lax.dynamic_slice_in_dim(query_blocks, head_start, group_heads, 3)
        do_part = lax.dynamic_slice_in_dim(out_blocks, head_start, group_heads, 3)
        source_parts = [
            lax.dynamic_slice_in_dim(source, head_start, group_heads, 3) for source in sources
        ]
        score_list = []
        views = []
        for source_id, offset, spread, valid_mask in pieces:
            block_count = blocks_here // spread
            key_blocks = source_parts[source_id][:, offset : offset + block_count]
            q_view = q_part.reshape(seqs_dev, block_count, spread, blk_rows, group_heads, head_size)
            do_view = do_part.reshape(
                seqs_dev, block_count, spread, blk_rows, group_heads, head_size
            )
            raw_scores = jnp.einsum(
                "bnrqhe,bnkhe->bnrhqk",
                q_view,
                key_blocks[..., 0, :],
                preferred_element_type=jnp.float32,
            )
            raw_scores = (
                raw_scores.reshape(seqs_dev, blocks_here, group_heads, blk_rows, blk_rows)
                * score_scale
            )
            score_list.append(
                jnp.where(valid_mask[None, :, None, None, None], raw_scores, -jnp.inf)
            )
            views.append((key_blocks, q_view, do_view, block_count, spread))
        all_scores = jnp.concatenate(score_list, 4)
        row_max = jnp.max(all_scores, 4, keepdims=True)
        exp_scores = jnp.exp(all_scores - row_max)
        summed = jnp.sum(exp_scores, 4, keepdims=True)
        prob_full = exp_scores / summed
        probs_low = prob_full.astype(jnp.bfloat16)
        attended_part = jnp.zeros(
            (seqs_dev, blocks_here, blk_rows, group_heads, head_size), jnp.float32
        )
        grad_prob_list = []
        for piece_id, (key_blocks, q_view, do_view, block_count, spread) in enumerate(views):
            p_slice = probs_low[..., piece_id * blk_rows : (piece_id + 1) * blk_rows].reshape(
                seqs_dev, block_count, spread, group_heads, blk_rows, blk_rows
            )
            attended_part = attended_part + jnp.einsum(
                "bnrhqk,bnkhe->bnrqhe",
                p_slice,
                key_blocks[..., 1, :],
                preferred_element_type=jnp.float32,
            ).reshape(attended_part.shape)
            grad_prob = jnp.einsum(
                "bnrqhe,bnkhe->bnrhqk",
                do_view,
                key_blocks[..., 1, :],
                preferred_element_type=jnp.float32,
            )
            grad_prob_list.append(
                grad_prob.reshape(seqs_dev, blocks_here, group_heads, blk_rows, blk_rows)
            )
        grad_prob_all = jnp.concatenate(grad_prob_list, 4)
        row_delta = jnp.sum(prob_full * grad_prob_all, 4, keepdims=True)
        dscore = (prob_full * (grad_prob_all - row_delta) * score_scale).astype(jnp.bfloat16)
        grad_q_part = jnp.zeros(
            (seqs_dev, blocks_here, blk_rows, group_heads, head_size), jnp.float32
        )
        group_grads = [jnp.zeros(part_arr.shape, jnp.float32) for part_arr in source_parts]
        for piece_id, (key_blocks, q_view, do_view, block_count, spread) in enumerate(views):
            source_id, offset = (pieces[piece_id][0], pieces[piece_id][1])
            p_slice = probs_low[..., piece_id * blk_rows : (piece_id + 1) * blk_rows].reshape(
                seqs_dev, block_count, spread, group_heads, blk_rows, blk_rows
            )
            ds_slice = dscore[..., piece_id * blk_rows : (piece_id + 1) * blk_rows].reshape(
                seqs_dev, block_count, spread, group_heads, blk_rows, blk_rows
            )
            grad_q_part = grad_q_part + jnp.einsum(
                "bnrhqk,bnkhe->bnrqhe",
                ds_slice,
                key_blocks[..., 0, :],
                preferred_element_type=jnp.float32,
            ).reshape(grad_q_part.shape)
            key_grad = jnp.einsum(
                "bnrhqk,bnrqhe->bnkhe", ds_slice, q_view, preferred_element_type=jnp.float32
            )
            value_grad = jnp.einsum(
                "bnrhqk,bnrqhe->bnkhe", p_slice, do_view, preferred_element_type=jnp.float32
            )
            pair_grad = jnp.stack([key_grad, value_grad], 4)
            group_grads[source_id] = (
                group_grads[source_id].at[:, offset : offset + block_count].add(pair_grad)
            )
        attended_acc = lax.dynamic_update_slice_in_dim(
            attended_acc, attended_part.astype(jnp.bfloat16), head_start, 3
        )
        grad_q_acc = lax.dynamic_update_slice_in_dim(
            grad_q_acc, grad_q_part.astype(jnp.bfloat16), head_start, 3
        )
        source_grads = tuple(
            (
                lax.dynamic_update_slice_in_dim(whole, group_part, head_start, 3)
                for whole, group_part in zip(source_grads, group_grads)
            )
        )
        log_totals = lax.dynamic_update_slice_in_dim(
            log_totals, (row_max + jnp.log(summed))[..., 0], head_start, 2
        )
        row_deltas = lax.dynamic_update_slice_in_dim(row_deltas, row_delta[..., 0], head_start, 2)
        return (attended_acc, grad_q_acc, source_grads, log_totals, row_deltas)

    start_state = (
        jnp.zeros((seqs_dev, blocks_here, blk_rows, head_count, head_size), jnp.bfloat16),
        jnp.zeros((seqs_dev, blocks_here, blk_rows, head_count, head_size), jnp.bfloat16),
        tuple((jnp.zeros(source.shape, jnp.float32) for source in sources)),
        jnp.zeros((seqs_dev, blocks_here, head_count, blk_rows), jnp.float32),
        jnp.zeros((seqs_dev, blocks_here, head_count, blk_rows), jnp.float32),
    )
    attended_acc, grad_q_acc, source_grads, log_totals, row_deltas = lax.fori_loop(
        0, head_count // group_heads, head_group, start_state
    )
    attended = attended_acc.reshape(seqs_dev, tok_rows, feat_width)
    grad_query = grad_q_acc.reshape(seqs_dev, tok_rows, feat_width)
    grad_left, grad_own, grad_right = ([], [], [])
    for level_id in range(local_top + 1):
        flat_grad = source_grads[level_id].reshape(seqs_dev, -1, pair_width)
        grad_left.append(flat_grad[:, :blk_rows])
        grad_own.append(flat_grad[:, blk_rows:-blk_rows])
        grad_right.append(flat_grad[:, -blk_rows:])
    group_left_grads = [
        source_grads[local_top + 1 + 2 * slot_id].reshape(seqs_dev, blk_rows, pair_width)
        for slot_id in range(levels - local_top)
    ]
    group_right_grads = [
        source_grads[local_top + 2 + 2 * slot_id].reshape(seqs_dev, blk_rows, pair_width)
        for slot_id in range(levels - local_top)
    ]
    weight_grads = [None] * levels
    carry_block = jnp.zeros((seqs_dev, blk_rows, pair_width), jnp.float32)
    carry_left = jnp.zeros((seqs_dev, 2, pair_width), jnp.float32)
    for level_id in range(levels, local_top, -1):
        slot_id = level_id - local_top - 1
        stride_dev = 2 ** (level_id - local_top)
        left_total = group_left_grads[slot_id].at[:, -2:].add(carry_left)
        block_total = (
            carry_block
            + move_grads(left_total, -stride_dev)
            + move_grads(group_right_grads[slot_id], stride_dev)
        )
        first_part = block_total[:, : blk_rows // 2]
        second_part = block_total[:, blk_rows // 2 :]
        keep_part = jnp.where(group_first[slot_id], first_part, second_part)
        give_part = jnp.where(group_first[slot_id], second_part, first_part)
        half_grad = keep_part + partner_2(give_part.astype(jnp.bfloat16), "seq", slot_id).astype(
            give_part.dtype
        )
        spread, weight_grads[level_id - 1] = coarsen_back(
            half_grad, group_extended[slot_id], kv_weight[level_id - 1]
        )
        carry_left = spread[:, :2]
        carry_block = spread[:, 2:]
    grad_left[local_top] = grad_left[local_top].at[:, -2:].add(carry_left)
    grad_own[local_top] = grad_own[local_top] + carry_block
    fine_left_conv = jnp.zeros((seqs_dev, blk_rows, pair_width), jnp.float32)
    level_id = 1
    from_right = move_grads(grad_left[level_id], -1)
    from_left = move_grads(grad_right[level_id], 1)
    level_grad = (
        grad_own[level_id].at[:, :blk_rows].add(from_left).at[:, -blk_rows:].add(from_right)
    )
    spread, weight_grads[level_id - 1] = coarsen_back(
        level_grad, extended_local[level_id], kv_weight[level_id - 1]
    )
    fine_left_conv = fine_left_conv.at[:, -2:].add(spread[:, :2])
    grad_own[level_id - 1] = grad_own[level_id - 1] + spread[:, 2:]
    from_right = move_grads(grad_left[0] + fine_left_conv, -1)
    from_left = move_grads(grad_right[0], 1)
    fine_grad = grad_own[0].at[:, :blk_rows].add(from_left).at[:, -blk_rows:].add(from_right)
    grad_pairs = fine_grad.reshape(seqs_dev, tok_rows, head_count, 2, head_size)
    grad_key = (
        grad_pairs[:, :, :, 0, :].reshape(seqs_dev, tok_rows, feat_width).astype(jnp.bfloat16)
    )
    grad_value = (
        grad_pairs[:, :, :, 1, :].reshape(seqs_dev, tok_rows, feat_width).astype(jnp.bfloat16)
    )
    weight_sum = lax.psum(jnp.stack(weight_grads), ("seq", "dp")).reshape(
        levels, 4, head_count, 2, head_size
    )
    grad_conv_key = weight_sum[:, :, :, 0, :].reshape(levels, 4, feat_width)
    grad_conv_value = weight_sum[:, :, :, 1, :].reshape(levels, 4, feat_width)
    return (attended, grad_query, grad_key, grad_value, grad_conv_key, grad_conv_value)


def solution(mesh):
    in_specs = (
        P("dp", "seq", None),
        P("dp", "seq", None),
        P("dp", "seq", None),
        P(),
        P(),
        P("dp", "seq", None),
    )
    out_specs = (
        P("dp", "seq", None),
        P("dp", "seq", None),
        P("dp", "seq", None),
        P("dp", "seq", None),
        P(),
        P(),
    )
    return jax.shard_map(
        per_device, mesh=mesh, in_specs=in_specs, out_specs=out_specs, check_vma=False
    )
```

profile of v0, /device:TPU:1, one launch (start us, length us, event | category | flops | bytes accessed | tf_op | source)
XLA Modules:
  0.0 1245.0 jit_solution(9767372504227561443)
XLA Ops:
  10.7 4.5 collective-permute-start
  15.2 20.2 %slice.1813 = bf16[1,128,2048]{1,2,0:T(8,128)(2,1)S(1)} slice(bf16[1,256,2048]{1,2,0:T(8,128)(2,1)S(1)} %bitcast.1716), slice={[0:1:1], [0:256:2], [0:2048:1]} | slice | bytes 1048576 | tf_op jit(solution)/shard_map/slice | solution.py:25
  35.5 20.2 %slice.1815 = bf16[1,128,2048]{1,2,0:T(8,128)(2,1)S(1)} slice(bf16[1,256,2048]{1,2,0:T(8,128)(2,1)S(1)} %bitcast.1717), slice={[0:1:1], [1:256:2], [0:2048:1]} | slice | bytes 1048576 | tf_op jit(solution)/shard_map/slice | solution.py:25
  58.7 20.9 %slice.1811 = bf16[1,128,2048]{1,2,0:T(8,128)(2,1)S(1)} slice(bf16[1,258,2048]{1,2,0:T(8,128)(2,1)} %pad_maximum_fusion.14), slice={[0:1:1], [1:257:2], [0:2048:1]} | slice | bytes 1048576 | tf_op jit(solution)/shard_map/slice | solution.py:25
  79.6 21.3 %slice.1809 = bf16[1,128,2048]{1,2,0:T(8,128)(2,1)} slice(bf16[1,258,2048]{1,2,0:T(8,128)(2,1)} %pad_maximum_fusion.14), slice={[0:1:1], [0:256:2], [0:2048:1]} | slice | bytes 1048576 | tf_op jit(solution)/shard_map/slice | solution.py:23
  106.1 11.0 slice.1824
  117.1 10.9 slice.1822
  130.9 11.6 slice.1820
  142.4 11.9 slice.1818
  166.5 11.0 slice.1833
  177.5 10.9 slice.1831
  191.2 11.9 slice.1829
  203.2 11.8 slice.1827
  218.9 12.9 %collective-permute-done.7 = bf16[1,64,2048]{1,2,0:T(8,128)(2,1)S(1)} collective-permute-done((bf16[1,64,2048]{1,2,0:T(8,128)(2,1)}, bf16[1,64,2048]{1,2,0:T(8,128)(2,1)S(1)}, u32[]{:S(2)}, u32[]{:S(2)}) %collective-permute-start.7) | collective-permute-done | bytes 262176 | tf_op jit(solution)/shard_map/ppermute | solution.py:18
  233.6 5.2 collective-permute-start.8
  238.8 11.0 slice.1842
  249.8 11.2 slice.1840
  263.7 11.9 slice.1838
  275.6 11.8 slice.1836
  287.4 4.0 fusion.185
  292.2 12.7 %collective-permute-done.10 = bf16[1,64,2048]{1,2,0:T(8,128)(2,1)S(1)} collective-permute-done((bf16[1,64,2048]{1,2,0:T(8,128)(2,1)}, bf16[1,64,2048]{1,2,0:T(8,128)(2,1)S(1)}, u32[]{:S(2)}, u32[]{:S(2)}) %collective-permute-start.10) | collective-permute-done | bytes 262176 | tf_op jit(solution)/shard_map/ppermute | solution.py:18
  310.9 4.8 collective-permute-start.1
  317.9 11.5 slice.1851
  329.4 11.8 slice.1849
  344.9 11.9 slice.1847
  356.9 11.8 slice.1845
  390.3 9.1 collective-permute-start.14
  426.1 424.3 %while.137 = (s32[]{:T(128)}, bf16[1,2,128,8,128]{4,3,2,1,0:T(8,128)(2,1)}, bf16[1,2,128,8,128]{4,3,2,1,0:T(8,128)(2,1)}, f32[1,4,128,8,2,128]{5,4,3,0,2,1:T(2,1...) while((s32[]{:T(128)}, ...), condition=%wide.region_16.17_spmd.clone.clone, body=%wide.region_0.16_spmd.clone.clone.sunk | while | flops 1327627008 | bytes 139415504 | solution.py:269
  851.7 5.8 scatter-add.44
  859.0 5.6 collective-permute-start.17
  864.6 7.6 collective-permute-done.16
  878.0 8.1 collective-permute-done.18
  893.3 6.1 scatter-add.45
  902.4 8.0 collective-permute-done.19
  912.0 13.4 %collective-permute-start.21 = (bf16[1,64,2048]{1,2,0:T(8,128)(2,1)S(1)}, bf16[1,64,2048]{1,2,0:T(8,128)(2,1)S(1)}, u32[]{:S(2)}, u32[]{:S(2)}) collective-permute-start(bf16[1,64,2048]{1,2,0:T(8,128)(2,1)S(1)} %select_convert_fusion.2), channel_id=1, source_target_pairs={{0,16},{4,20},{8,24},{12,28},{16,0},{20,4},{24,8},{28,12},{32,48},... | collective-permute-start | bytes 786440 | tf_op jit(solution)/shard_map/ppermute | solution.py:18
  928.3 4.6 collective-permute-done.21
  940.1 6.1 scatter-add.46
  949.2 9.5 collective-permute-done.22
  960.3 9.3 collective-permute-start.24
  988.1 8.6 scatter-add.49
  1001.5 5.7 collective-permute-done.25
  1009.6 17.7 %collective-permute-start.27 = (bf16[1,64,2048]{1,2,0:T(8,128)(2,1)}, bf16[1,64,2048]{1,2,0:T(8,128)(2,1)}, u32[]{:S(2)}, u32[]{:S(2)}) collective-permute-start(bf16[1,64,2048]{1,2,0:T(8,128)(2,1)} %select_convert_fusion), channel_id=1, source_target_pairs={{0,4},{4,0},{8,12},{12,8},{16,20},{20,16},{24,28},{28,24},{32,36},... | collective-permute-start | bytes 786440 | tf_op jit(solution)/shard_map/ppermute | solution.py:18
  1042.5 4.5 collective-permute-start.28
  1047.0 4.5 slice.2068
  1059.1 5.8 scatter-add.50
  1071.4 4.2 collective-permute-start.30
  1089.2 5.5 copy.821
  1102.5 129.7 %all-reduce.24.cloned.1.call-done = f32[5,4,8,2,128]{4,3,2,1,0:T(2,128)} async-done(((f32[5,4,8,2,128]{4,3,2,1,0:T(2,128)}), f32[5,4,8,2,128]{4,3,2,1,0:T(2,128)}) %all-reduce.24.cloned.1.call-update) | async-done | bytes 163856 | tf_op jit(solution)/shard_map/psum | solution.py:336
  (1171 shorter events, 635.0 us)
Async XLA Ops:
  7.2 1225.0 %all-reduce.24.cloned.1.call-start = ((), (), s32[]{:S(2)}) async-start(), calls=%async_computation | async-start | bytes 327680 | tf_op jit(solution)/shard_map/psum | solution.py:336
  10.7 45.3 %collective-permute-start = (bf16[1,128,2048]{1,2,0:T(8,128)(2,1)S(1)}, bf16[1,128,2048]{1,2,0:T(8,128)(2,1)S(1)}, u32[]{:S(2)}, u32[]{:S(2)}) collective-permute-start(bf16[1,128,2048]{1,2,0:T(8,128)(2,1)S(1)} %get-tuple-element.1887), channel_id=1, source_target_pairs={{0,4},{4,8},{8,12},{12,16},{16,20},{20,24},{24,28},{28,32},{32,36}... | collective-permute-start | bytes 1572872 | tf_op jit(solution)/shard_map/ppermute | solution.py:14
  35.5 65.5 %copy-start.38 = (bf16[1,128,2048]{1,2,0:T(8,128)(2,1)}, bf16[1,128,2048]{1,2,0:T(8,128)(2,1)S(1)}, u32[]{:S(2)}) copy-start(bf16[1,128,2048]{1,2,0:T(8,128)(2,1)S(1)} %slice.1813) | copy-start | bytes 1572868
  55.9 98.4 %copy-start.86 = (f32[1,1,8,2,128]{4,3,2,1,0:T(2,128)}, f32[1,1,8,2,128]{4,3,2,1,0:T(2,128)S(1)}, u32[]{:S(2)}) copy-start(f32[1,1,8,2,128]{4,3,2,1,0:T(2,128)S(1)} %get-tuple-element.1899) | copy-start | bytes 24580
  56.0 98.4 %copy-start.88 = (f32[1,1,8,2,128]{4,3,2,1,0:T(2,128)}, f32[1,1,8,2,128]{4,3,2,1,0:T(2,128)S(1)}, u32[]{:S(2)}) copy-start(f32[1,1,8,2,128]{4,3,2,1,0:T(2,128)S(1)} %get-tuple-element.1900) | copy-start | bytes 24580
  56.0 98.4 %copy-start.90 = (f32[1,1,8,2,128]{4,3,2,1,0:T(2,128)}, f32[1,1,8,2,128]{4,3,2,1,0:T(2,128)S(1)}, u32[]{:S(2)}) copy-start(f32[1,1,8,2,128]{4,3,2,1,0:T(2,128)S(1)} %get-tuple-element.1901) | copy-start | bytes 24580
  56.0 98.4 %copy-start.92 = (f32[1,1,8,2,128]{4,3,2,1,0:T(2,128)}, f32[1,1,8,2,128]{4,3,2,1,0:T(2,128)S(1)}, u32[]{:S(2)}) copy-start(f32[1,1,8,2,128]{4,3,2,1,0:T(2,128)S(1)} %get-tuple-element.1902) | copy-start | bytes 24580
  56.0 312.6 %copy-start.102 = (f32[1,1,8,2,128]{4,3,2,1,0:T(2,128)}, f32[1,1,8,2,128]{4,3,2,1,0:T(2,128)S(1)}, u32[]{:S(2)}) copy-start(f32[1,1,8,2,128]{4,3,2,1,0:T(2,128)S(1)} %get-tuple-element.1894) | copy-start | bytes 24580
  103.9 24.1 %collective-permute-start.2 = (bf16[1,128,2048]{1,2,0:T(8,128)(2,1)S(1)}, bf16[1,128,2048]{1,2,0:T(8,128)(2,1)}, u32[]{:S(2)}, u32[]{:S(2)}) collective-permute-start(bf16[1,128,2048]{1,2,0:T(8,128)(2,1)S(1)} %fusion.161), channel_id=1, source_target_pairs={{0,4},{4,8},{8,12},{12,16},{16,20},{20,24},{24,28},{28,32},{32,36}... | collective-permute-start | bytes 1572872 | tf_op jit(solution)/shard_map/ppermute | solution.py:14
  158.0 3.0 collective-permute-start.4
  162.9 25.5 %collective-permute-start.5 = (bf16[1,128,2048]{1,2,0:T(8,128)(2,1)S(1)}, bf16[1,128,2048]{1,2,0:T(8,128)(2,1)}, u32[]{:S(2)}, u32[]{:S(2)}) collective-permute-start(bf16[1,128,2048]{1,2,0:T(8,128)(2,1)S(1)} %maximum_select_fusion), channel_id=1, source_target_pairs={{0,8},{4,12},{8,16},{12,20},{16,24},{20,28},{24,32},{28,36},{32,40... | collective-permute-start | bytes 1572872 | tf_op jit(solution)/shard_map/ppermute | solution.py:14
  166.4 48.6 %copy-start.94 = (f32[1,1,8,2,128]{4,3,2,1,0:T(2,128)}, f32[1,1,8,2,128]{4,3,2,1,0:T(2,128)S(1)}, u32[]{:S(2)}) copy-start(f32[1,1,8,2,128]{4,3,2,1,0:T(2,128)S(1)} %get-tuple-element.1904) | copy-start | bytes 24580
  166.4 48.6 %copy-start.96 = (f32[1,1,8,2,128]{4,3,2,1,0:T(2,128)}, f32[1,1,8,2,128]{4,3,2,1,0:T(2,128)S(1)}, u32[]{:S(2)}) copy-start(f32[1,1,8,2,128]{4,3,2,1,0:T(2,128)S(1)} %get-tuple-element.1905) | copy-start | bytes 24580
  166.4 48.5 %copy-start.98 = (f32[1,1,8,2,128]{4,3,2,1,0:T(2,128)}, f32[1,1,8,2,128]{4,3,2,1,0:T(2,128)S(1)}, u32[]{:S(2)}) copy-start(f32[1,1,8,2,128]{4,3,2,1,0:T(2,128)S(1)} %get-tuple-element.1906) | copy-start | bytes 24580
  166.4 121.0 %copy-start.104 = (f32[1,1,8,2,128]{4,3,2,1,0:T(2,128)}, f32[1,1,8,2,128]{4,3,2,1,0:T(2,128)S(1)}, u32[]{:S(2)}) copy-start(f32[1,1,8,2,128]{4,3,2,1,0:T(2,128)S(1)} %get-tuple-element.1908) | copy-start | bytes 24580
  166.4 121.0 %copy-start.106 = (f32[1,1,8,2,128]{4,3,2,1,0:T(2,128)}, f32[1,1,8,2,128]{4,3,2,1,0:T(2,128)S(1)}, u32[]{:S(2)}) copy-start(f32[1,1,8,2,128]{4,3,2,1,0:T(2,128)S(1)} %get-tuple-element.1909) | copy-start | bytes 24580
  166.4 121.0 %copy-start.108 = (f32[1,1,8,2,128]{4,3,2,1,0:T(2,128)}, f32[1,1,8,2,128]{4,3,2,1,0:T(2,128)S(1)}, u32[]{:S(2)}) copy-start(f32[1,1,8,2,128]{4,3,2,1,0:T(2,128)S(1)} %get-tuple-element.1910) | copy-start | bytes 24580
  166.4 121.0 %copy-start.110 = (f32[1,1,8,2,128]{4,3,2,1,0:T(2,128)}, f32[1,1,8,2,128]{4,3,2,1,0:T(2,128)S(1)}, u32[]{:S(2)}) copy-start(f32[1,1,8,2,128]{4,3,2,1,0:T(2,128)S(1)} %get-tuple-element.1911) | copy-start | bytes 24580
  166.4 202.2 %copy-start.112 = (f32[1,1,8,2,128]{4,3,2,1,0:T(2,128)}, f32[1,1,8,2,128]{4,3,2,1,0:T(2,128)S(1)}, u32[]{:S(2)}) copy-start(f32[1,1,8,2,128]{4,3,2,1,0:T(2,128)S(1)} %get-tuple-element.1903) | copy-start | bytes 24580
  218.8 13.0 %collective-permute-start.7 = (bf16[1,64,2048]{1,2,0:T(8,128)(2,1)}, bf16[1,64,2048]{1,2,0:T(8,128)(2,1)S(1)}, u32[]{:S(2)}, u32[]{:S(2)}) collective-permute-start(bf16[1,64,2048]{1,2,0:T(8,128)(2,1)} %fusion.177), channel_id=1, source_target_pairs={{0,8},{4,12},{8,0},{12,4},{16,24},{20,28},{24,16},{28,20},{32,40},... | collective-permute-start | bytes 786440 | tf_op jit(solution)/shard_map/ppermute | solution.py:18
  233.6 27.5 %collective-permute-start.8 = (bf16[1,128,2048]{1,2,0:T(8,128)(2,1)S(1)}, bf16[1,128,2048]{1,2,0:T(8,128)(2,1)}, u32[]{:S(2)}, u32[]{:S(2)}) collective-permute-start(bf16[1,128,2048]{1,2,0:T(8,128)(2,1)S(1)} %maximum_select_fusion.1), channel_id=1, source_target_pairs={{0,16},{4,20},{8,24},{12,28},{16,32},{20,36},{24,40},{28,44},{32,4... | collective-permute-start | bytes 1572872 | tf_op jit(solution)/shard_map/ppermute | solution.py:14
  291.4 13.4 %collective-permute-start.10 = (bf16[1,64,2048]{1,2,0:T(8,128)(2,1)}, bf16[1,64,2048]{1,2,0:T(8,128)(2,1)S(1)}, u32[]{:S(2)}, u32[]{:S(2)}) collective-permute-start(bf16[1,64,2048]{1,2,0:T(8,128)(2,1)} %fusion.185), channel_id=1, source_target_pairs={{0,16},{4,20},{8,24},{12,28},{16,0},{20,4},{24,8},{28,12},{32,48},... | collective-permute-start | bytes 786440 | tf_op jit(solution)/shard_map/ppermute | solution.py:18
  307.4 33.8 %collective-permute-start.11 = (bf16[1,128,2048]{1,2,0:T(8,128)(2,1)}, bf16[1,128,2048]{1,2,0:T(8,128)(2,1)}, u32[]{:S(2)}, u32[]{:S(2)}) collective-permute-start(bf16[1,128,2048]{1,2,0:T(8,128)(2,1)} %maximum_select_fusion.2), channel_id=1, source_target_pairs={{0,32},{4,36},{8,40},{12,44},{16,48},{20,52},{24,56},{28,60},{32,6... | collective-permute-start | bytes 1572872 | tf_op jit(solution)/shard_map/ppermute | solution.py:14
  310.9 78.1 %collective-permute-start.1 = (bf16[1,128,2048]{1,2,0:T(8,128)(2,1)}, bf16[1,128,2048]{1,2,0:T(8,128)(2,1)}, u32[]{:S(2)}, u32[]{:S(2)}) collective-permute-start(bf16[1,128,2048]{1,2,0:T(8,128)(2,1)} %get-tuple-element.1888), channel_id=1, source_target_pairs={{4,0},{8,4},{12,8},{16,12},{20,16},{24,20},{28,24},{32,28},{36,32}... | collective-permute-start | bytes 1572872 | tf_op jit(solution)/shard_map/ppermute | solution.py:14
  315.8 52.8 %copy-start.76 = (f32[1,1,8,2,128]{4,3,2,1,0:T(2,128)}, f32[1,1,8,2,128]{4,3,2,1,0:T(2,128)S(1)}, u32[]{:S(2)}) copy-start(f32[1,1,8,2,128]{4,3,2,1,0:T(2,128)S(1)} %get-tuple-element.1913) | copy-start | bytes 24580
  315.8 74.5 %collective-permute-start.3 = (bf16[1,128,2048]{1,2,0:T(8,128)(2,1)S(1)}, bf16[1,128,2048]{1,2,0:T(8,128)(2,1)}, u32[]{:S(2)}, u32[]{:S(2)}) collective-permute-start(bf16[1,128,2048]{1,2,0:T(8,128)(2,1)S(1)} %fusion.161), channel_id=1, source_target_pairs={{4,0},{8,4},{12,8},{16,12},{20,16},{24,20},{28,24},{32,28},{36,32}... | collective-permute-start | bytes 1572872 | tf_op jit(solution)/shard_map/ppermute | solution.py:14
  372.6 12.1 collective-permute-start.13
  380.5 34.4 %collective-permute-start.6 = (bf16[1,128,2048]{1,2,0:T(8,128)(2,1)S(1)}, bf16[1,128,2048]{1,2,0:T(8,128)(2,1)}, u32[]{:S(2)}, u32[]{:S(2)}) collective-permute-start(bf16[1,128,2048]{1,2,0:T(8,128)(2,1)S(1)} %maximum_select_fusion), channel_id=1, source_target_pairs={{8,0},{12,4},{16,8},{20,12},{24,16},{28,20},{32,24},{36,28},{40,32... | collective-permute-start | bytes 1572872 | tf_op jit(solution)/shard_map/ppermute | solution.py:14
  381.8 33.1 %collective-permute-start.9 = (bf16[1,128,2048]{1,2,0:T(8,128)(2,1)S(1)}, bf16[1,128,2048]{1,2,0:T(8,128)(2,1)}, u32[]{:S(2)}, u32[]{:S(2)}) collective-permute-start(bf16[1,128,2048]{1,2,0:T(8,128)(2,1)S(1)} %maximum_select_fusion.1), channel_id=1, source_target_pairs={{16,0},{20,4},{24,8},{28,12},{32,16},{36,20},{40,24},{44,28},{48,3... | collective-permute-start | bytes 1572872 | tf_op jit(solution)/shard_map/ppermute | solution.py:14
  384.7 30.2 %collective-permute-start.12 = (bf16[1,128,2048]{1,2,0:T(8,128)(2,1)}, bf16[1,128,2048]{1,2,0:T(8,128)(2,1)}, u32[]{:S(2)}, u32[]{:S(2)}) collective-permute-start(bf16[1,128,2048]{1,2,0:T(8,128)(2,1)} %maximum_select_fusion.2), channel_id=1, source_target_pairs={{32,0},{36,4},{40,8},{44,12},{48,16},{52,20},{56,24},{60,28},{64,3... | collective-permute-start | bytes 1572872 | tf_op jit(solution)/shard_map/ppermute | solution.py:14
  389.0 25.9 %collective-permute-start.15 = (bf16[1,128,2048]{1,2,0:T(8,128)(2,1)}, bf16[1,128,2048]{1,2,0:T(8,128)(2,1)}, u32[]{:S(2)}, u32[]{:S(2)}) collective-permute-start(bf16[1,128,2048]{1,2,0:T(8,128)(2,1)} %maximum_select_fusion.3), channel_id=1, source_target_pairs={{64,0},{68,4},{72,8},{76,12},{80,16},{84,20},{88,24},{92,28},{96,3... | collective-permute-start | bytes 1572872 | tf_op jit(solution)/shard_map/ppermute | solution.py:14
  390.3 24.6 %collective-permute-start.14 = (bf16[1,128,2048]{1,2,0:T(8,128)(2,1)}, bf16[1,128,2048]{1,2,0:T(8,128)(2,1)}, u32[]{:S(2)}, u32[]{:S(2)}) collective-permute-start(bf16[1,128,2048]{1,2,0:T(8,128)(2,1)} %maximum_select_fusion.3), channel_id=1, source_target_pairs={{0,64},{4,68},{8,72},{12,76},{16,80},{20,84},{24,88},{28,92},{32,9... | collective-permute-start | bytes 1572872 | tf_op jit(solution)/shard_map/ppermute | solution.py:14
  857.6 14.6 %collective-permute-start.16 = (bf16[1,128,2048]{1,2,0:T(8,128)(2,1)}, bf16[1,128,2048]{1,2,0:T(8,128)(2,1)S(1)}, u32[]{:S(2)}, u32[]{:S(2)}) collective-permute-start(bf16[1,128,2048]{1,2,0:T(8,128)(2,1)} %scatter-add.44), channel_id=1, source_target_pairs={{64,0},{68,4},{72,8},{76,12},{80,16},{84,20},{88,24},{92,28},{96,3... | collective-permute-start | bytes 1572872 | tf_op jit(solution)/shard_map/ppermute | solution.py:14
  859.0 13.9 %collective-permute-start.17 = (bf16[1,128,2048]{1,2,0:T(8,128)(2,1)S(1)}, bf16[1,128,2048]{1,2,0:T(8,128)(2,1)S(1)}, u32[]{:S(2)}, u32[]{:S(2)}) collective-permute-start(bf16[1,128,2048]{1,2,0:T(8,128)(2,1)S(1)} %bitcast.1758), channel_id=1, source_target_pairs={{0,64},{4,68},{8,72},{12,76},{16,80},{20,84},{24,88},{28,92},{32,9... | collective-permute-start | bytes 1572872 | tf_op jit(solution)/shard_map/ppermute | solution.py:14
  873.2 12.9 %collective-permute-start.18 = (bf16[1,64,2048]{1,2,0:T(8,128)(2,1)S(1)}, bf16[1,64,2048]{1,2,0:T(8,128)(2,1)S(1)}, u32[]{:S(2)}, u32[]{:S(2)}) collective-permute-start(bf16[1,64,2048]{1,2,0:T(8,128)(2,1)S(1)} %select_convert_fusion.3), channel_id=1, source_target_pairs={{0,32},{4,36},{8,40},{12,44},{16,48},{20,52},{24,56},{28,60},{32,0... | collective-permute-start | bytes 786440 | tf_op jit(solution)/shard_map/ppermute | solution.py:18
  875.1 27.3 %collective-permute-start.20 = (bf16[1,128,2048]{1,2,0:T(8,128)(2,1)}, bf16[1,128,2048]{1,2,0:T(8,128)(2,1)}, u32[]{:S(2)}, u32[]{:S(2)}) collective-permute-start(bf16[1,128,2048]{1,2,0:T(8,128)(2,1)} %bitcast.41), channel_id=1, source_target_pairs={{0,32},{4,36},{8,40},{12,44},{16,48},{20,52},{24,56},{28,60},{32,6... | collective-permute-start | bytes 1572872 | tf_op jit(solution)/shard_map/ppermute | solution.py:14
  900.2 10.2 collective-permute-start.19
  912.0 20.8 %collective-permute-start.21 = (bf16[1,64,2048]{1,2,0:T(8,128)(2,1)S(1)}, bf16[1,64,2048]{1,2,0:T(8,128)(2,1)S(1)}, u32[]{:S(2)}, u32[]{:S(2)}) collective-permute-start(bf16[1,64,2048]{1,2,0:T(8,128)(2,1)S(1)} %select_convert_fusion.2), channel_id=1, source_target_pairs={{0,16},{4,20},{8,24},{12,28},{16,0},{20,4},{24,8},{28,12},{32,48},... | collective-permute-start | bytes 786440 | tf_op jit(solution)/shard_map/ppermute | solution.py:18
  925.4 23.9 %collective-permute-start.23 = (bf16[1,128,2048]{1,2,0:T(8,128)(2,1)}, bf16[1,128,2048]{1,2,0:T(8,128)(2,1)}, u32[]{:S(2)}, u32[]{:S(2)}) collective-permute-start(bf16[1,128,2048]{1,2,0:T(8,128)(2,1)} %bitcast.46), channel_id=1, source_target_pairs={{0,16},{4,20},{8,24},{12,28},{16,32},{20,36},{24,40},{28,44},{32,4... | collective-permute-start | bytes 1572872 | tf_op jit(solution)/shard_map/ppermute | solution.py:14
  947.0 11.7 collective-permute-start.22
  960.3 15.9 %collective-permute-start.24 = (bf16[1,64,2048]{1,2,0:T(8,128)(2,1)S(1)}, bf16[1,64,2048]{1,2,0:T(8,128)(2,1)S(1)}, u32[]{:S(2)}, u32[]{:S(2)}) collective-permute-start(bf16[1,64,2048]{1,2,0:T(8,128)(2,1)S(1)} %select_convert_fusion.1), channel_id=1, source_target_pairs={{0,8},{4,12},{8,0},{12,4},{16,24},{20,28},{24,16},{28,20},{32,40},... | collective-permute-start | bytes 786440 | tf_op jit(solution)/shard_map/ppermute | solution.py:18
  969.7 31.8 %collective-permute-start.26 = (bf16[1,128,2048]{1,2,0:T(8,128)(2,1)S(1)}, bf16[1,128,2048]{1,2,0:T(8,128)(2,1)}, u32[]{:S(2)}, u32[]{:S(2)}) collective-permute-start(bf16[1,128,2048]{1,2,0:T(8,128)(2,1)S(1)} %bitcast.1723), channel_id=1, source_target_pairs={{0,8},{4,12},{8,16},{12,20},{16,24},{20,28},{24,32},{28,36},{32,40... | collective-permute-start | bytes 1572872 | tf_op jit(solution)/shard_map/ppermute | solution.py:14
  996.8 10.4 collective-permute-start.25
  1009.6 41.9 %collective-permute-start.27 = (bf16[1,64,2048]{1,2,0:T(8,128)(2,1)}, bf16[1,64,2048]{1,2,0:T(8,128)(2,1)}, u32[]{:S(2)}, u32[]{:S(2)}) collective-permute-start(bf16[1,64,2048]{1,2,0:T(8,128)(2,1)} %select_convert_fusion), channel_id=1, source_target_pairs={{0,4},{4,0},{8,12},{12,8},{16,20},{20,16},{24,28},{28,24},{32,36},... | collective-permute-start | bytes 786440 | tf_op jit(solution)/shard_map/ppermute | solution.py:18
  1042.5 37.8 %collective-permute-start.28 = (bf16[1,128,2048]{1,2,0:T(8,128)(2,1)}, bf16[1,128,2048]{1,2,0:T(8,128)(2,1)}, u32[]{:S(2)}, u32[]{:S(2)}) collective-permute-start(bf16[1,128,2048]{1,2,0:T(8,128)(2,1)} %copy.1124), channel_id=1, source_target_pairs={{0,4},{4,8},{8,12},{12,16},{16,20},{20,24},{24,28},{28,32},{32,36}... | collective-permute-start | bytes 1572872 | tf_op jit(solution)/shard_map/ppermute | solution.py:14
  1064.9 15.4 %collective-permute-start.29 = (bf16[1,128,2048]{1,2,0:T(8,128)(2,1)}, bf16[1,128,2048]{1,2,0:T(8,128)(2,1)}, u32[]{:S(2)}, u32[]{:S(2)}) collective-permute-start(bf16[1,128,2048]{1,2,0:T(8,128)(2,1)} %scatter-add.50), channel_id=1, source_target_pairs={{4,0},{8,4},{12,8},{16,12},{20,16},{24,20},{28,24},{32,28},{36,32}... | collective-permute-start | bytes 1572872 | tf_op jit(solution)/shard_map/ppermute | solution.py:14
  1071.4 29.8 %collective-permute-start.30 = (bf16[1,128,2048]{2,1,0:T(8,128)(2,1)}, bf16[1,128,2048]{2,1,0:T(8,128)(2,1)}, u32[]{:S(2)}, u32[]{:S(2)}) collective-permute-start(bf16[1,128,2048]{2,1,0:T(8,128)(2,1)} %copy.823), channel_id=1, source_target_pairs={{0,4},{4,8},{8,12},{12,16},{16,20},{20,24},{24,28},{28,32},{32,36}... | collective-permute-start | bytes 1572872 | tf_op jit(solution)/shard_map/ppermute | solution.py:14
  1097.3 137.7 %collective-permute-start.31 = (bf16[1,128,2048]{2,1,0:T(8,128)(2,1)S(1)}, bf16[1,128,2048]{2,1,0:T(8,128)(2,1)S(1)}, u32[]{:S(2)}, u32[]{:S(2)}) collective-permute-start(bf16[1,128,2048]{2,1,0:T(8,128)(2,1)S(1)} %copy.824), channel_id=1, source_target_pairs={{4,0},{8,4},{12,8},{16,12},{20,16},{24,20},{28,24},{32,28},{36,32}... | collective-permute-start | bytes 1572872 | tf_op jit(solution)/shard_map/ppermute | solution.py:14
  (236 other events, 2402.6 us)
Sparse Core Ops, SparseCore 0:
  1084.6 147.5 all-reduce.23
where the time goes:
time: 1260 us; the launch traced here: 1240 us
  local copies, waits for them, and re-layouts  460 us (37%)
  matrix products  290 us (23%)
  waiting for transfers between devices  207 us (16%)
  other arithmetic  151 us (12%)
  starting transfers between devices  117 us (9%)
  between operations  16 us (1%)
    slice x15, local copies, waits for them, and re-layouts, coarsen(): extended[:, offset:offset + 2 * out_rows:2].astype(jnp.float32)  198 us
    psum x1, waiting for transfers between devices, per_device(): lax.psum(jnp.stack(weight_grads), ('seq', 'dp'))  130 us
    dot_general x52, matrix products, head_group(): jnp.einsum('bnrqhe,bnkhe->bnrhqk', q_view, key_blocks[..., 0, :], preferr...  75.9 us
    ppermute x24, starting transfers between devices, passed_along(): lax.ppermute(value, axis, [(source, source + steps) for source in range(i...  72 us
    slice x5, local copies, waits for them, and re-layouts, coarsen(): summed = weight[0] * extended[:, 0:2 * out_rows:2].astype(jnp.float32)  68.5 us
    dot_general x52, matrix products, head_group(): jnp.einsum('bnrhqk,bnkhe->bnrqhe', p_slice, key_blocks[..., 1, :], prefer...  50.2 us
    dot_general x52, matrix products, head_group(): jnp.einsum('bnrqhe,bnkhe->bnrhqk', do_view, key_blocks[..., 1, :], prefer...  45.6 us
    ppermute x8, waiting for transfers between devices, partner_2(): lax.ppermute(array, axis, [(i, i ^ 1 << distance) for i in range(lax.axis...  45.3 us
  transfers between devices with their start and end apart: 33, of which 13 were waited for; matrix products, arithmetic and copies ran while one was open for 25% of the time, Pallas kernels for 0%

commit v1 on v0

v1 whole, which is shorter than its diff:
```python
import functools
import math

import jax
import jax.numpy as jnp
from jax import lax
from jax.experimental import pallas as pl
from jax.experimental.pallas import tpu as pltpu
from jax.sharding import Mesh, PartitionSpec as P

HD = 128
BLK = 128
LEVELS = 5
NZ, NX, NC, NY = 4, 4, 2, 4
ROWS = 256
GROUP = ROWS * NX * NC
PAIRS = GROUP // 256
SIZES = [GROUP >> l for l in range(LEVELS + 1)]
HALO = [64 >> l for l in range(LEVELS + 1)]
PRE = 8
OFFS = [0]
for _l in range(LEVELS):
    OFFS.append(OFFS[-1] + SIZES[_l] + 2 * BLK)
TOTAL = OFFS[LEVELS] + BLK
NBLK = TOTAL // BLK
KEYS = 4 * BLK + 8 * BLK + BLK
SCALE = HD ** -0.5
EXPC = SCALE * math.log2(math.e)
NEG = -1e30
F32 = jnp.float32
BF16 = jnp.bfloat16
PARAMS = pltpu.CompilerParams(vmem_limit_bytes=56 << 20)


def nn(a, b):
    return lax.dot_general(a, b, (((1,), (0,)), ((), ())), preferred_element_type=F32)


def nt(a, b):
    return lax.dot_general(a, b, (((1,), (1,)), ((), ())), preferred_element_type=F32)


def chunks(total, step):
    return [(r, min(step, total - r)) for r in range(0, total, step)]


def coarse_kernel(z_ref, *refs):
    srcs, halos, weights = refs[0:2], refs[2:4], refs[4:6]
    outs = refs[6:]
    has_left = (z_ref[0] > 0).astype(F32)
    per = LEVELS * 2
    for side in range(2):
        src, halo, weight = srcs[side], halos[side], weights[side]
        wide = outs[side * per : side * per + LEVELS]
        own = outs[side * per + LEVELS : (side + 1) * per]
        x = wide[0]
        x[0:PRE, :] = jnp.zeros((PRE, HD), F32)
        x[PRE : PRE + HALO[0], :] = halo[...].astype(F32) * has_left
        for r, n in chunks(GROUP, 256):
            x[PRE + HALO[0] + r : PRE + HALO[0] + r + n, :] = src[r : r + n, :].astype(F32)
        for level in range(1, LEVELS + 1):
            x = wide[level - 1]
            taps = [weight[4 * (level - 1) + j : 4 * (level - 1) + j + 1, :] for j in range(4)]
            if level < LEVELS:
                wide[level][0:PRE, :] = jnp.zeros((PRE, HD), F32)
            first = 0 if level < LEVELS else HALO[level]
            for r, n in chunks(HALO[level] + SIZES[level] - first, 128):
                r += first
                acc = None
                for j in range(4):
                    term = taps[j] * x[pl.ds(PRE + 2 * r - 2 + j, n, stride=2), :]
                    acc = term if acc is None else acc + term
                low = acc.astype(BF16)
                if level < LEVELS:
                    wide[level][PRE + r : PRE + r + n, :] = low.astype(F32)
                else:
                    own[level - 1][r - first : r - first + n, :] = low
            if level < LEVELS:
                for r, n in chunks(SIZES[level], 256):
                    start = PRE + HALO[level] + r
                    own[level - 1][r : r + n, :] = wide[level][start : start + n, :].astype(BF16)


def attention_kernel(z_ref, q_ref, do_ref, *refs):
    own_k = refs[0:LEVELS]
    own_v = refs[LEVELS : 2 * LEVELS]
    rim_l, rim_r, far = refs[2 * LEVELS : 2 * LEVELS + 3]
    att_ref, dq_ref, gl_ref, gr_ref, gfar_ref, dk_ref, dv_ref = refs[2 * LEVELS + 3 : 2 * LEVELS + 10]
    kx, vx, kt, vt, s_ref, e_ref = refs[2 * LEVELS + 10 :]
    z = z_ref[0]
    for side, (own, ext, tr, grad) in enumerate(((own_k, kx, kt, dk_ref), (own_v, vx, vt, dv_ref))):
        for level in range(LEVELS):
            off = OFFS[level]
            ext[off : off + BLK, :] = rim_l[level, side]
            for r, n in chunks(SIZES[level], 256):
                ext[off + BLK + r : off + BLK + r + n, :] = own[level][r : r + n, :]
            end = off + BLK + SIZES[level]
            ext[end : end + BLK, :] = rim_r[level, side]
        ext[OFFS[LEVELS] : TOTAL, :] = far[side]

        def prepare(i, _, ext=ext, tr=tr, grad=grad):
            rows = pl.ds(pl.multiple_of(i * BLK, BLK), BLK)
            tr[i] = ext[rows, :].T
            grad[rows, :] = jnp.zeros((BLK, HD), F32)
            return 0

        lax.fori_loop(0, NBLK, prepare, 0)

    lane = lax.broadcasted_iota(jnp.int32, (BLK, 2 * BLK), 1)

    def pair(p, _):
        qrows = pl.ds(pl.multiple_of(p * 256, 256), 256)
        qt = q_ref[qrows, :].T
        dot_t = do_ref[qrows, :].astype(F32).T
        groups = [[2 * p + i for i in range(4)]]
        valid = [None]
        for level in range(1, LEVELS):
            c = p >> (level - 1)
            base = OFFS[level] // BLK
            groups.append([base + c, base + c + 2])
            count = SIZES[level] // BLK
            valid.append((jnp.logical_or(c > 0, z > 0), jnp.logical_or(c < count - 1, z < NZ - 1)))
        groups.append([OFFS[LEVELS] // BLK])
        valid.append((None,))

        def rows_of(ext, blocks, contiguous):
            if contiguous:
                return ext[pl.ds(pl.multiple_of(blocks[0] * BLK, BLK), BLK * len(blocks)), :]
            parts = [ext[pl.ds(pl.multiple_of(b * BLK, BLK), BLK), :] for b in blocks]
            return parts[0] if len(parts) == 1 else jnp.concatenate(parts, 0)

        def cols_of(tr, blocks):
            parts = [tr[b] for b in blocks]
            return parts[0] if len(parts) == 1 else jnp.concatenate(parts, 1)

        top = jnp.full((8, 256), NEG, F32)
        row = 0
        for gid, blocks in enumerate(groups):
            n = BLK * len(blocks)
            s = nn(rows_of(kx, blocks, gid == 0), qt)
            for i in range(len(blocks)):
                part = s[i * BLK : (i + 1) * BLK, :]
                if gid == 0 and i == 0:
                    lim = jnp.where(jnp.logical_or(p > 0, z > 0), BLK, 0)
                    part = jnp.where(lane < lim, part, NEG)
                elif gid == 0 and i == 3:
                    lim = jnp.where(jnp.logical_or(p < PAIRS - 1, z < NZ - 1), BLK, 2 * BLK)
                    part = jnp.where(lane >= lim, part, NEG)
                elif gid > 0 and valid[gid][i] is not None:
                    part = jnp.where(valid[gid][i], part, NEG)
                s_ref[row + i * BLK : row + (i + 1) * BLK, :] = part
                top = jnp.maximum(top, jnp.max(part.reshape(BLK // 8, 8, 256), 0))
            row += n
        shift = jnp.max(top, 0, keepdims=True) * EXPC
        total = jnp.zeros((8, 256), F32)
        out_t = jnp.zeros((HD, 256), F32)
        row = 0
        for gid, blocks in enumerate(groups):
            n = BLK * len(blocks)
            e = jnp.exp2(s_ref[row : row + n, :] * EXPC - shift)
            total = total + jnp.sum(e.reshape(n // 8, 8, 256), 0)
            low = e.astype(BF16)
            e_ref[row : row + n, :] = low
            out_t = out_t + nn(cols_of(vt, blocks), low)
            row += n
        inverse = 1.0 / jnp.sum(total, 0, keepdims=True)
        out_t = out_t * inverse
        att_ref[qrows, :] = out_t.T.astype(BF16)
        don_t = (dot_t * inverse).astype(BF16)
        delta = jnp.sum(don_t.astype(F32) * out_t, 0, keepdims=True)
        dq_t = jnp.zeros((HD, 256), F32)
        row = 0
        for gid, blocks in enumerate(groups):
            n = BLK * len(blocks)
            low = e_ref[row : row + n, :]
            dp = nn(rows_of(vx, blocks, gid == 0), don_t)
            ds = (low.astype(F32) * (dp - delta)).astype(BF16)
            dq_t = dq_t + nn(cols_of(kt, blocks), ds)
            dk = nt(ds, qt)
            dv = nt(low, don_t)
            for i, b in enumerate(blocks):
                rows = pl.ds(pl.multiple_of(b * BLK, BLK), BLK)
                dk_ref[rows, :] += dk[i * BLK : (i + 1) * BLK, :]
                dv_ref[rows, :] += dv[i * BLK : (i + 1) * BLK, :]
            row += n
        dq_ref[qrows, :] = (dq_t * SCALE).T.astype(BF16)
        return 0

    lax.fori_loop(0, PAIRS, pair, 0)
    for level in range(LEVELS):
        off = OFFS[level]
        end = off + BLK + SIZES[level]
        gl_ref[level, 0] = (dk_ref[off : off + BLK, :] * SCALE).astype(BF16)
        gl_ref[level, 1] = dv_ref[off : off + BLK, :].astype(BF16)
        gr_ref[level, 0] = (dk_ref[end : end + BLK, :] * SCALE).astype(BF16)
        gr_ref[level, 1] = dv_ref[end : end + BLK, :].astype(BF16)
    gfar_ref[0] = (dk_ref[OFFS[LEVELS] : TOTAL, :] * SCALE).astype(BF16)
    gfar_ref[1] = dv_ref[OFFS[LEVELS] : TOTAL, :].astype(BF16)


def back_kernel(dk_ref, dv_ref, from_left, from_right, far_a, far_b, wk_ref, wv_ref, *refs):
    xs = (refs[0:LEVELS], refs[LEVELS : 2 * LEVELS])
    fine_outs, halo_out, gw_outs = refs[2 * LEVELS : 2 * LEVELS + 2], refs[2 * LEVELS + 2], refs[2 * LEVELS + 3 : 2 * LEVELS + 5]
    g = refs[2 * LEVELS + 5 :]
    for side in range(2):
        weight = (wk_ref, wv_ref)[side]
        grad = (dk_ref, dv_ref)[side]
        mult = (SCALE, 1.0)[side]
        fine_out, gw_out = fine_outs[side], gw_outs[side]
        end = HALO[LEVELS] + SIZES[LEVELS]
        g[LEVELS][0 : HALO[LEVELS], :] = jnp.zeros((HALO[LEVELS], HD), F32)
        g[LEVELS][HALO[LEVELS] : end, :] = far_a[side].astype(F32) + far_b[side].astype(F32)
        g[LEVELS][end : end + 8, :] = jnp.zeros((8, HD), F32)
        for level in range(LEVELS, 0, -1):
            taps = [weight[4 * (level - 1) + j : 4 * (level - 1) + j + 1, :] for j in range(4)]
            x = xs[side][level - 1]
            here, below = g[level], g[level - 1]
            sums = [jnp.zeros((8, HD), F32) for _ in range(4)]
            total = HALO[level] + SIZES[level]
            for r, n in chunks(total, 128):
                g0 = here[r : r + n, :]
                g1 = here[r + 1 : r + n + 1, :]
                below[pl.ds(2 * r, n, stride=2), :] = taps[2] * g0 + taps[0] * g1
                below[pl.ds(2 * r + 1, n, stride=2), :] = taps[3] * g0 + taps[1] * g1
                for j in range(4):
                    prod = g0 * x[pl.ds(PRE + 2 * r - 2 + j, n, stride=2), :]
                    if n % 8 == 0:
                        sums[j] = sums[j] + jnp.sum(prod.reshape(n // 8, 8, HD), 0)
                    else:
                        gap = jnp.zeros((8 - n % 8, HD), F32)
                        prod = jnp.concatenate([prod, gap], 0)
                        sums[j] = sums[j] + jnp.sum(prod.reshape((n + 7) // 8, 8, HD), 0)
            for j in range(4):
                gw_out[4 * (level - 1) + j : 4 * (level - 1) + j + 1, :] = jnp.sum(sums[j], 0, keepdims=True)
            low = level - 1
            off = OFFS[low] + BLK
            size, pad = SIZES[low], HALO[low]
            for r, n in chunks(size, 128):
                value = below[pad + r : pad + r + n, :] + grad[off + r : off + r + n, :] * mult
                if r == 0:
                    value = value + from_left[low, side].astype(F32)
                if r == size - BLK:
                    value = value + from_right[low, side].astype(F32)
                if low > 0:
                    below[pad + r : pad + r + n, :] = value
                else:
                    fine_out[r : r + n, :] = value.astype(BF16)
            if low > 0:
                below[pad + size : pad + size + 8, :] = jnp.zeros((8, HD), F32)
            else:
                halo_out[side] = below[0:pad, :].astype(BF16)


def ring(axis, k, size=4):
    return [(i, (i + k) % size) for i in range(size)]


def swap_core(value):
    return lax.ppermute(value, "c", [(0, 1), (1, 0)])


def take(value, index, dim):
    return lax.dynamic_index_in_dim(value, index, dim, keepdims=False)


def rows_to_heads(arrays):
    n = len(arrays)
    x, c = lax.axis_index("x"), lax.axis_index("c")
    stacked = jnp.stack([a.reshape(ROWS, NX, NC, HD) for a in arrays], 0)
    by_head = stacked.transpose(2, 3, 0, 1, 4)
    keep, give = take(by_head, c, 1), take(by_head, 1 - c, 1)
    got = swap_core(give)
    both = jnp.stack([jnp.where(c == 0, keep, got), jnp.where(c == 0, got, keep)], 2)
    whole = jnp.zeros((n, NX, NC, ROWS, HD), BF16)
    for k in (0, 1, 3, 2):
        piece = take(both, (x + k) % NX, 0)
        if k:
            piece = lax.ppermute(piece, "x", ring("x", k))
        whole = lax.dynamic_update_slice_in_dim(whole, piece[:, None], (x - k) % NX, 1)
    return [whole[i].reshape(GROUP, HD) for i in range(n)]


def heads_to_rows(arrays):
    n = len(arrays)
    x, c = lax.axis_index("x"), lax.axis_index("c")
    stacked = jnp.stack([a.reshape(NX, NC, ROWS, HD) for a in arrays], 1)
    whole = jnp.zeros((NX, n, NC, ROWS, HD), BF16)
    for k in (0, 1, 3, 2):
        piece = take(stacked, (x + k) % NX, 0)
        if k:
            piece = lax.ppermute(piece, "x", ring("x", k))
        whole = lax.dynamic_update_slice_in_dim(whole, piece[None], (x - k) % NX, 0)
    keep, give = take(whole, c, 2), take(whole, 1 - c, 2)
    got = swap_core(give)
    both = jnp.stack([jnp.where(c == 0, keep, got), jnp.where(c == 0, got, keep)], 1)
    rows = both.transpose(2, 3, 0, 1, 4).reshape(n, ROWS, NX * NC * HD)
    return [rows[i] for i in range(n)]


def up(value):
    return lax.ppermute(value, "z", [(i, i + 1) for i in range(NZ - 1)])


def down(value):
    return lax.ppermute(value, "z", [(i + 1, i) for i in range(NZ - 1)])


def across(value, flip):
    return lax.ppermute(value, "z", [(i, i ^ flip) for i in range(NZ)])


def sum_over(value, axis):
    return value + sum(lax.ppermute(value, axis, ring(axis, k)) for k in (1, 2, 3))


def smem():
    return pl.BlockSpec(memory_space=pltpu.SMEM)


def vmem():
    return pl.BlockSpec(memory_space=pltpu.VMEM)


def sds(shape, dtype):
    return jax.ShapeDtypeStruct(shape, dtype)


def per_device(queries, key_rows, value_rows, conv_key, conv_value, grad_out):
    z, x, c = lax.axis_index("z"), lax.axis_index("x"), lax.axis_index("c")
    head = x * NC + c
    zs = z.astype(jnp.int32).reshape(1)
    wk = lax.dynamic_slice_in_dim(conv_key, head * HD, HD, 2).reshape(4 * LEVELS, HD)
    wv = lax.dynamic_slice_in_dim(conv_value, head * HD, HD, 2).reshape(4 * LEVELS, HD)
    k0, v0 = rows_to_heads([key_rows[0], value_rows[0]])
    fine_l = up(jnp.stack([k0[-BLK:], v0[-BLK:]], 0))
    fine_r = down(jnp.stack([k0[:BLK], v0[:BLK]], 0))

    wide_shapes = [sds((PRE + HALO[l] + SIZES[l], HD), F32) for l in range(LEVELS)]
    own_shapes = [sds((SIZES[l], HD), BF16) for l in range(1, LEVELS + 1)]
    made = pl.pallas_call(
        coarse_kernel,
        out_shape=(wide_shapes + own_shapes) * 2,
        in_specs=[smem()] + [vmem()] * 6,
        out_specs=[vmem()] * (4 * LEVELS),
        compiler_params=PARAMS,
        name="coarsen",
    )(zs, k0, v0, fine_l[0, BLK - HALO[0] :], fine_l[1, BLK - HALO[0] :], wk, wv)
    wide_k, own_k = made[:LEVELS], made[LEVELS : 2 * LEVELS]
    wide_v, own_v = made[2 * LEVELS : 3 * LEVELS], made[3 * LEVELS :]

    coarse_l = up(jnp.stack([jnp.stack([own_k[i][-BLK:], own_v[i][-BLK:]], 0) for i in range(LEVELS - 1)], 0))
    coarse_r = down(jnp.stack([jnp.stack([own_k[i][:BLK], own_v[i][:BLK]], 0) for i in range(LEVELS - 1)], 0))
    last = jnp.stack([own_k[-1], own_v[-1]], 0)
    far = jnp.concatenate([across(last, 2), across(last, 3)], 1)
    q, do = rows_to_heads([queries[0], grad_out[0]])
    rim_l = jnp.concatenate([fine_l[None], coarse_l], 0)
    rim_r = jnp.concatenate([fine_r[None], coarse_r], 0)

    outs = pl.pallas_call(
        attention_kernel,
        out_shape=[
            sds((GROUP, HD), BF16),
            sds((GROUP, HD), BF16),
            sds((LEVELS, 2, BLK, HD), BF16),
            sds((LEVELS, 2, BLK, HD), BF16),
            sds((2, BLK, HD), BF16),
            sds((TOTAL, HD), F32),
            sds((TOTAL, HD), F32),
        ],
        in_specs=[smem()] + [vmem()] * (2 + 2 * LEVELS + 3),
        out_specs=[vmem()] * 7,
        scratch_shapes=[
            pltpu.VMEM((TOTAL, HD), BF16),
            pltpu.VMEM((TOTAL, HD), BF16),
            pltpu.VMEM((NBLK, HD, BLK), BF16),
            pltpu.VMEM((NBLK, HD, BLK), BF16),
            pltpu.VMEM((KEYS, 256), F32),
            pltpu.VMEM((KEYS, 256), BF16),
        ],
        compiler_params=PARAMS,
        name="attend",
    )(zs, q, do, k0, *own_k[:4], v0, *own_v[:4], rim_l, rim_r, far)
    att, dq, g_left, g_right, g_far, dk, dv = outs
    from_right = down(g_left)
    from_left = up(g_right)
    half = SIZES[LEVELS]
    far_a = across(g_far[:, :half], 2)
    far_b = across(g_far[:, half:], 3)
    attended, grad_query = heads_to_rows([att, dq])

    made = pl.pallas_call(
        back_kernel,
        out_shape=[
            sds((GROUP, HD), BF16),
            sds((GROUP, HD), BF16),
            sds((2, HALO[0], HD), BF16),
            sds((4 * LEVELS, HD), F32),
            sds((4 * LEVELS, HD), F32),
        ],
        in_specs=[vmem()] * (8 + 2 * LEVELS),
        out_specs=[vmem()] * 5,
        scratch_shapes=[pltpu.VMEM((HALO[l] + SIZES[l] + 8, HD), F32) for l in range(LEVELS + 1)],
        compiler_params=PARAMS,
        name="coarsen_back",
    )(dk, dv, from_left, from_right, far_a, far_b, wk, wv, *wide_k, *wide_v)
    gk, gv, halo, gwk, gwv = made
    halo = down(halo)
    gk = gk.at[-HALO[0] :].add(halo[0])
    gv = gv.at[-HALO[0] :].add(halo[1])
    grad_key, grad_value = heads_to_rows([gk, gv])

    gw = sum_over(sum_over(jnp.stack([gwk, gwv], 0), "z"), "y")
    whole = jnp.zeros((NX, 2, 4 * LEVELS, HD), F32)
    for k in range(NX):
        piece = lax.ppermute(gw, "x", ring("x", k)) if k else gw
        whole = lax.dynamic_update_slice_in_dim(whole, piece[None], (x - k) % NX, 0)
    other = swap_core(whole)
    both = jnp.stack([jnp.where(c == 0, whole, other), jnp.where(c == 0, other, whole)], 1)
    both = both.transpose(2, 3, 0, 1, 4).reshape(2, LEVELS, 4, NX * NC * HD)
    return attended[None], grad_query[None], grad_key[None], grad_value[None], both[0], both[1]


def solution(mesh):
    split = Mesh(mesh.devices.reshape(NZ, NX, NC, NY), ("z", "x", "c", "y"))
    rows = P("y", ("z", "x", "c"), None)
    return jax.shard_map(
        per_device,
        mesh=split,
        in_specs=(rows, rows, rows, P(), P(), rows),
        out_specs=(rows, rows, rows, rows, P(), P()),
        check_vma=False,
    )
```

time: 1260 us -> 190 us (0.15); the launches traced: 1240 us -> 189 us
  local copies, waits for them, and re-layouts: 460 us -> 30.8 us
  matrix products: 290 us -> 0 us
  waiting for transfers between devices: 207 us -> 27.3 us
  other arithmetic: 151 us -> 14.8 us
  starting transfers between devices: 117 us -> 72.6 us
  Pallas kernels: 0 us -> 41.8 us
  between operations: 16 us -> 1.39 us
    slice x46 -> x12, local copies, waits for them, and re-layouts: 300 us -> 2.43 us  [the longest x2 1.11 us: rows_to_heads(): return [whole[i].reshape(GROUP, HD) for i in range(n)]]
    dot_general x312 -> x0, matrix products: 290 us -> none  [the longest x52 75.9 us: head_group(): jnp.einsum('bnrqhe,bnkhe->bnrhqk', q_view, key_blocks[..., 0, :], preferr...]
    psum x1 -> x0, waiting for transfers between devices: 130 us -> none  [per_device(): lax.psum(jnp.stack(weight_grads), ('seq', 'dp'))]
    ppermute x32 -> x37, waiting for transfers between devices: 76.9 us -> 27.3 us  [the longest x6 13 us: rows_to_heads(): piece = lax.ppermute(piece, 'x', ring('x', k))]
    ppermute x32 -> x37, starting transfers between devices: 117 us -> 72.6 us  [the longest x5 18.1 us: swap_core(): return lax.ppermute(value, 'c', [(0, 1), (1, 0)])]
    pallas_call x0 -> x3, Pallas kernels: none -> 41.8 us  [the longest x1 31.8 us: per_device(): pl.pallas_call(attention_kernel, out_shape=[sds((GROUP, HD), BF16), sds((...]
    scatter-add x5 -> x0, local copies, waits for them, and re-layouts: 32.4 us -> none  [the longest x4 26.6 us: per_device(): left_total = group_left_grads[slot_id].at[:, -2:].add(carry_left)]
    convert_element_type x16 -> x0, other arithmetic: 25.9 us -> none  [the longest x5 18.3 us: coarsen(): return summed.astype(jnp.bfloat16)]
  transfers between devices with their start and end apart: 33 -> 37, of which waited for: 13 -> 10; matrix products, arithmetic and copies ran while one was open for 25% -> 19% of each run, Pallas kernels for 0% -> 2%
where the time goes in v1:
time: 190 us; the launch traced here: 189 us
  starting transfers between devices  72.6 us (38%)
  Pallas kernels  41.8 us (22%)
  local copies, waits for them, and re-layouts  30.8 us (16%)
  waiting for transfers between devices  27.3 us (14%)
  other arithmetic  14.8 us (8%)
    pallas_call x1, Pallas kernels, per_device(): pl.pallas_call(attention_kernel, out_shape=[sds((GROUP, HD), BF16), sds((...  31.8 us
    ppermute x5, starting transfers between devices, swap_core(): return lax.ppermute(value, 'c', [(0, 1), (1, 0)])  18.1 us
    ppermute x6, waiting for transfers between devices, rows_to_heads(): piece = lax.ppermute(piece, 'x', ring('x', k))  13 us
    ppermute x3, starting transfers between devices, up(): return lax.ppermute(value, 'z', [(i, i + 1) for i in range(NZ - 1)])  11.4 us
    ppermute x4, starting transfers between devices, across(): return lax.ppermute(value, 'z', [(i, i ^ flip) for i in range(NZ)])  9.21 us
    ppermute x3, waiting for transfers between devices, per_device(): piece = lax.ppermute(gw, 'x', ring('x', k)) if k else gw  8.38 us
    ppermute x6, starting transfers between devices, sum_over(): lax.ppermute(value, axis, ring(axis, k))  7.88 us
    unnamed x24, local copies, waits for them, and re-layouts  7.83 us
  transfers between devices with their start and end apart: 37, of which 10 were waited for; matrix products, arithmetic and copies ran while one was open for 19% of the time, Pallas kernels for 2%

profile of v1, /device:TPU:1, one launch (start us, length us, event | category | flops | bytes accessed | tf_op | source)
XLA Modules:
  0.0 188.7 jit_solution(8305188531034826179)
XLA Ops:
  0.7 1.3 copy.44
  2.0 1.2 copy.45
  4.1 1.4 collective-permute-start
  9.9 1.3 collective-permute-start.1
  12.1 1.4 collective-permute-start.2
  14.3 1.6 collective-permute-start.3
  18.3 2.4 %collective-permute-start.6 = (bf16[2,2,256,128]{3,2,1,0:T(8,128)(2,1)}, bf16[2,2,256,128]{3,2,1,0:T(8,128)(2,1)S(1)}, u32[]{:S(2)}, u32[]{:S(2)}) collective-permute-start(bf16[2,2,256,128]{3,2,1,0:T(8,128)(2,1)} %bitcast.35), channel_id=1, source_target_pairs={{0,24},{8,0},{16,8},{24,16},{1,25},{9,1},{17,9},{25,17},{2,26},{10... | collective-permute-start | bytes 786440 | tf_op jit(solution)/shard_map/ppermute | solution.py:278
  22.5 9.4 %collective-permute-done.5 = bf16[2,2,256,128]{3,2,1,0:T(8,128)(2,1)} collective-permute-done((bf16[2,2,256,128]{3,2,1,0:T(8,128)(2,1)}, bf16[2,2,256,128]{3,2,1,0:T(8,128)(2,1)}, u32[]{:S(2)}, u32[]{:S(2)}) %collective-permute-start.5) | collective-permute-done | bytes 262176 | tf_op jit(solution)/shard_map/ppermute | solution.py:278
  33.0 3.7 %collective-permute-done.7 = bf16[2,2,256,128]{3,2,1,0:T(8,128)(2,1)S(1)} collective-permute-done((bf16[2,2,256,128]{3,2,1,0:T(8,128)(2,1)S(1)}, bf16[2,2,256,128]{3,2,1,0:T(8,128)(2,1)S(1)}, u32[]{:S(2)}, u32[]{:S(2)}) %collective-permute-start.7) | collective-permute-done | bytes 262176 | tf_op jit(solution)/shard_map/ppermute | solution.py:278
  36.9 3.5 %collective-permute-start.8 = (bf16[2,128,128]{2,1,0:T(8,128)(2,1)S(1)}, bf16[2,128,128]{2,1,0:T(8,128)(2,1)S(1)}, u32[]{:S(2)}, u32[]{:S(2)}) collective-permute-start(bf16[2,128,128]{2,1,0:T(8,128)(2,1)S(1)} %pad_maximum_fusion.4), channel_id=1, source_target_pairs={{0,32},{32,64},{64,96},{1,33},{33,65},{65,97},{2,34},{34,66},{66,9... | collective-permute-start | bytes 196616 | tf_op jit(solution)/shard_map/ppermute | solution.py:301
  40.5 1.3 collective-permute-start.10
  42.4 3.8 %coarsen.1 = (f32[2120,128]{1,0:T(8,128)}, f32[1064,128]{1,0:T(8,128)}, f32[536,128]{1,0:T(8,128)}, f32[272,128]{1,0:T(8,128)}, f32[140,128]{1,0:T(8,128)}, /*in...) custom-call(s32[1]{0:T(128)} %bitcast.z_ref, ...), custom_call_target="tpu_custom_call" | custom-call | tf_op jit(solution)/shard_map/coarsen/pallas_call | solution.py:340
  46.9 4.0 %collective-permute-start.12 = (bf16[2,64,128]{2,1,0:T(8,128)(2,1)S(1)}, bf16[2,64,128]{2,1,0:T(8,128)(2,1)S(1)}, u32[]{:S(2)}, u32[]{:S(2)}) collective-permute-start(bf16[2,64,128]{2,1,0:T(8,128)(2,1)S(1)} %pad_maximum_fusion.7), channel_id=1, source_target_pairs={{0,64},{32,96},{64,0},{96,32},{1,65},{33,97},{65,1},{97,33},{2,66}... | collective-permute-start | bytes 98312 | tf_op jit(solution)/shard_map/ppermute | solution.py:309
  57.2 1.3 collective-permute-start.11
  58.5 4.0 %collective-permute-start.9 = (bf16[4,2,128,128]{3,2,1,0:T(8,128)(2,1)S(1)}, bf16[4,2,128,128]{3,2,1,0:T(8,128)(2,1)S(1)}, u32[]{:S(2)}, u32[]{:S(2)}) collective-permute-start(bf16[4,2,128,128]{3,2,1,0:T(8,128)(2,1)S(1)} %get-tuple-element.151), channel_id=1, source_target_pairs={{0,32},{32,64},{64,96},{1,33},{33,65},{65,97},{2,34},{34,66},{66,9... | collective-permute-start | bytes 786440 | tf_op jit(solution)/shard_map/ppermute | solution.py:301
  62.5 1.0 fusion.41
  66.5 31.8 %attend.1 = (bf16[2048,128]{1,0:T(8,128)(2,1)}, bf16[2048,128]{1,0:T(8,128)(2,1)}, bf16[5,2,128,128]{3,2,1,0:T(8,128)(2,1)}, bf16[5,2,128,128]{3,2,1,0:T(8,128)(...) custom-call(s32[1]{0:T(128)} %bitcast.z_ref, bf16[2048,128]{1,0:T(8,128)(2,1)} %bitcast.244, ...), custom_call_target="tpu_custom_call" | custom-call | tf_op jit(solution)/shard_map/attend/pallas_call | solution.py:359
  98.3 3.8 %collective-permute-start.18 = (bf16[5,2,128,128]{3,2,1,0:T(8,128)(2,1)}, bf16[5,2,128,128]{3,2,1,0:T(8,128)(2,1)S(1)}, u32[]{:S(2)}, u32[]{:S(2)}) collective-permute-start(bf16[5,2,128,128]{3,2,1,0:T(8,128)(2,1)} %get-tuple-element.76), channel_id=1, source_target_pairs={{0,32},{32,64},{64,96},{1,33},{33,65},{65,97},{2,34},{34,66},{66,9... | collective-permute-start | bytes 983048 | tf_op jit(solution)/shard_map/ppermute | solution.py:301
  102.1 1.3 collective-permute-start.19
  103.4 1.4 fusion.20
  105.0 1.8 collective-permute-start.14
  109.5 2.0 %collective-permute-done.14 = bf16[2,2,256,128]{3,2,1,0:T(8,128)(2,1)S(1)} collective-permute-done((bf16[2,2,256,128]{3,2,1,0:T(8,128)(2,1)S(1)}, bf16[2,2,256,128]{3,2,1,0:T(8,128)(2,1)S(1)}, u32[]{:S(2)}, u32[]{:S(2)}) %collective-permute-start.14) | collective-permute-done | bytes 262176 | tf_op jit(solution)/shard_map/ppermute | solution.py:291
  111.5 2.8 %collective-permute-start.20 = (bf16[2,64,128]{2,1,0:T(8,128)(2,1)S(1)}, bf16[2,64,128]{2,1,0:T(8,128)(2,1)S(1)}, u32[]{:S(2)}, u32[]{:S(2)}) collective-permute-start(bf16[2,64,128]{2,1,0:T(8,128)(2,1)S(1)} %get-tuple-element.149), channel_id=1, source_target_pairs={{0,64},{32,96},{64,0},{96,32},{1,65},{33,97},{65,1},{97,33},{2,66}... | collective-permute-start | bytes 98312 | tf_op jit(solution)/shard_map/ppermute | solution.py:309
  114.5 1.7 collective-permute-start.21
  116.6 2.2 %collective-permute-done.21.far_b = bf16[2,64,128]{2,1,0:T(8,128)(2,1)S(1)} collective-permute-done((bf16[2,64,128]{2,1,0:T(8,128)(2,1)S(1)}, bf16[2,64,128]{2,1,0:T(8,128)(2,1)S(1)}, u32[]{:S(2)}, u32[]{:S(2)}) %collective-permute-start.21) | collective-permute-done | bytes 32800 | tf_op jit(solution)/shard_map/ppermute | solution.py:309
  119.7 6.3 %coarsen_back.1 = (bf16[2048,128]{1,0:T(8,128)(2,1)}, bf16[2048,128]{1,0:T(8,128)(2,1)}, bf16[2,64,128]{2,1,0:T(8,128)(2,1)}, f32[20,128]{1,0:T(8,128)}, f32[20,128]{1,0:T(8,128)}) custom-call(f32[5376,128]{1,0:T(8,128)} %get-tuple-element.74.dk_ref, f32[5376,128]{1,0:T(8,128)} %get-tuple-element.75.dv_ref, bf16[5,2,128,128]{3,2,1,0:T(8,128)(2,1)} %copy-done.4, ...), custom_call_target="tpu_custom_call" | custom-call | tf_op jit(solution)/shard_map/coarsen_back/pallas_call | solution.py:391
  126.7 2.8 %collective-permute-start.28 = (f32[2,20,128]{2,1,0:T(8,128)S(1)}, f32[2,20,128]{2,1,0:T(8,128)S(1)}, u32[]{:S(2)}, u32[]{:S(2)}) collective-permute-start(f32[2,20,128]{2,1,0:T(8,128)S(1)} %pad_maximum_fusion.8), channel_id=1, source_target_pairs={{0,64},{32,96},{64,0},{96,32},{1,65},{33,97},{65,1},{97,33},{2,66}... | collective-permute-start | bytes 61448 | tf_op jit(solution)/shard_map/ppermute | solution.py:313
  129.5 8.9 %collective-permute-start.17 = (bf16[4,2,256,128]{2,3,0,1:T(8,128)(2,1)S(1)}, bf16[4,2,256,128]{2,3,0,1:T(8,128)(2,1)}, u32[]{:S(2)}, u32[]{:S(2)}) collective-permute-start(bf16[4,2,256,128]{2,3,0,1:T(8,128)(2,1)S(1)} %dynamic-slice_bitcast_fusion.1), channel_id=1, source_target_pairs={{0,4},{4,0},{1,5},{5,1},{2,6},{6,2},{3,7},{7,3},{8,12},{12,8},{9,1... | collective-permute-start | bytes 1572872 | tf_op jit(solution)/shard_map/ppermute | solution.py:259
  138.4 1.3 collective-permute-start.22
  140.5 1.4 collective-permute-start.30
  141.8 2.6 %collective-permute-start.31 = (f32[2,20,128]{2,1,0:T(8,128)S(1)}, f32[2,20,128]{2,1,0:T(8,128)S(1)}, u32[]{:S(2)}, u32[]{:S(2)}) collective-permute-start(f32[2,20,128]{2,1,0:T(8,128)S(1)} %add_add_fusion.1), channel_id=1, source_target_pairs={{0,2},{1,3},{2,0},{3,1},{4,6},{5,7},{6,4},{7,5},{8,10},{9,11},{10,... | collective-permute-start | bytes 61448 | tf_op jit(solution)/shard_map/ppermute | solution.py:313
  144.5 1.1 collective-permute-start.32
  145.5 1.4 constant_dynamic-update-slice_fusion.4
  146.9 2.2 %fusion.13 = (bf16[2,2,256,128]{3,2,1,0:T(8,128)(2,1)S(1)}, bf16[1,2,2,256,128]{4,3,2,1,0:T(8,128)(2,1)S(1)}, bf16[2,2,256,128]{3,2,1,0:T(8,128)(2,1)}, bf16[2,2,256,128]{3,2,1,0:T(8,128)(2,1)}) fusion(s32[]{:T(128)S(6)} %select_n.222, bf16[4,1,2,256,128]{4,3,2,1,0:T(8,128)(2,1)} %bitcast.245, bf16[4,1,2,256,128]{4,3,2,1,0:T(8,128)(2,1)} %bitcast.246, ...), kind=kLoop, calls=%fused_computation.69 | loop fusion | flops 524288 | bytes 2097168 | tf_op jit(solution)/shard_map/jit(dynamic_index_in_dim)/squeeze | solution.py:263
  149.3 2.7 %collective-permute-start.24 = (bf16[2,2,256,128]{3,2,1,0:T(8,128)(2,1)}, bf16[2,2,256,128]{3,2,1,0:T(8,128)(2,1)}, u32[]{:S(2)}, u32[]{:S(2)}) collective-permute-start(bf16[2,2,256,128]{3,2,1,0:T(8,128)(2,1)} %get-tuple-element.113), channel_id=1, source_target_pairs={{0,24},{8,0},{16,8},{24,16},{1,25},{9,1},{17,9},{25,17},{2,26},{10... | collective-permute-start | bytes 786440 | tf_op jit(solution)/shard_map/ppermute | solution.py:291
  152.8 5.6 %collective-permute-done.33 = f32[2,20,128]{2,1,0:T(8,128)S(1)} collective-permute-done((f32[2,20,128]{2,1,0:T(8,128)S(1)}, f32[2,20,128]{2,1,0:T(8,128)S(1)}, u32[]{:S(2)}, u32[]{:S(2)}) %collective-permute-start.33) | collective-permute-done | bytes 20512 | tf_op jit(solution)/shard_map/ppermute | solution.py:415
  158.4 3.2 %collective-permute-start.34 = (f32[2,20,128]{2,1,0:T(8,128)S(1)}, f32[2,20,128]{2,1,0:T(8,128)S(1)}, u32[]{:S(2)}, u32[]{:S(2)}) collective-permute-start(f32[2,20,128]{2,1,0:T(8,128)S(1)} %add_add_fusion), channel_id=1, source_target_pairs={{0,16},{8,24},{16,0},{24,8},{1,17},{9,25},{17,1},{25,9},{2,18},{10... | collective-permute-start | bytes 61448 | tf_op jit(solution)/shard_map/ppermute | solution.py:415
  161.6 1.9 collective-permute-done.34
  163.5 3.4 %collective-permute-start.35 = (f32[2,20,128]{2,1,0:T(8,128)S(1)}, f32[2,20,128]{2,1,0:T(8,128)S(1)}, u32[]{:S(2)}, u32[]{:S(2)}) collective-permute-start(f32[2,20,128]{2,1,0:T(8,128)S(1)} %add_add_fusion), channel_id=1, source_target_pairs={{0,24},{8,0},{16,8},{24,16},{1,25},{9,1},{17,9},{25,17},{2,26},{10... | collective-permute-start | bytes 61448 | tf_op jit(solution)/shard_map/ppermute | solution.py:415
  167.9 7.4 %collective-permute-start.36 = (f32[4,2,20,128]{3,1,2,0:T(2,128)S(1)}, f32[4,2,20,128]{3,1,2,0:T(2,128)S(1)}, u32[]{:S(2)}, u32[]{:S(2)}) collective-permute-start(f32[4,2,20,128]{3,1,2,0:T(2,128)S(1)} %copy_dynamic-update-slice_fusion), channel_id=1, source_target_pairs={{0,4},{4,0},{1,5},{5,1},{2,6},{6,2},{3,7},{7,3},{8,12},{12,8},{9,1... | collective-permute-start | bytes 245768 | tf_op jit(solution)/shard_map/ppermute | solution.py:259
  178.0 1.1 copy.78
  179.1 1.1 copy.79
  180.2 1.1 copy.80
  181.9 1.1 fusion.10
  183.2 1.0 copy.91
  185.3 1.1 fusion.8
  186.6 1.0 copy.93
  187.7 1.0 copy.94
  (153 shorter events, 35.4 us)
Async XLA Ops:
  0.6 4.8 %copy-start.2 = (bf16[1,256,1024]{2,1,0:T(8,128)(2,1)S(1)}, bf16[1,256,1024]{2,1,0:T(8,128)(2,1)}, u32[]{:S(2)}) copy-start(bf16[1,256,1024]{2,1,0:T(8,128)(2,1)} %param.11) | copy-start | bytes 1572868
  0.6 5.0 %copy-start.3 = (bf16[1,256,1024]{2,1,0:T(8,128)(2,1)S(1)}, bf16[1,256,1024]{2,1,0:T(8,128)(2,1)}, u32[]{:S(2)}) copy-start(bf16[1,256,1024]{2,1,0:T(8,128)(2,1)} %param.12) | copy-start | bytes 1572868
  4.1 4.6 %collective-permute-start = (bf16[4,2,256,128]{2,3,0,1:T(8,128)(2,1)}, bf16[4,2,256,128]{2,3,0,1:T(8,128)(2,1)S(1)}, u32[]{:S(2)}, u32[]{:S(2)}) collective-permute-start(bf16[4,2,256,128]{2,3,0,1:T(8,128)(2,1)} %fusion.5), channel_id=1, source_target_pairs={{0,4},{4,0},{1,5},{5,1},{2,6},{6,2},{3,7},{7,3},{8,12},{12,8},{9,1... | collective-permute-start | bytes 1572872 | tf_op jit(solution)/shard_map/ppermute | solution.py:259
  6.8 9.2 %collective-permute-start.4 = (bf16[4,2,256,128]{2,3,0,1:T(8,128)(2,1)}, bf16[4,2,256,128]{2,3,0,1:T(8,128)(2,1)S(1)}, u32[]{:S(2)}, u32[]{:S(2)}) collective-permute-start(bf16[4,2,256,128]{2,3,0,1:T(8,128)(2,1)} %fusion.1), channel_id=1, source_target_pairs={{0,4},{4,0},{1,5},{5,1},{2,6},{6,2},{3,7},{7,3},{8,12},{12,8},{9,1... | collective-permute-start | bytes 1572872 | tf_op jit(solution)/shard_map/ppermute | solution.py:259
  9.9 11.4 %collective-permute-start.1 = (bf16[2,2,256,128]{3,2,1,0:T(8,128)(2,1)}, bf16[2,2,256,128]{3,2,1,0:T(8,128)(2,1)}, u32[]{:S(2)}, u32[]{:S(2)}) collective-permute-start(bf16[2,2,256,128]{3,2,1,0:T(8,128)(2,1)} %bitcast.11), channel_id=1, source_target_pairs={{0,8},{8,16},{16,24},{24,0},{1,9},{9,17},{17,25},{25,1},{2,10},{10... | collective-permute-start | bytes 786440 | tf_op jit(solution)/shard_map/ppermute | solution.py:278
  12.1 20.8 %collective-permute-start.2 = (bf16[2,2,256,128]{3,2,1,0:T(8,128)(2,1)}, bf16[2,2,256,128]{3,2,1,0:T(8,128)(2,1)S(1)}, u32[]{:S(2)}, u32[]{:S(2)}) collective-permute-start(bf16[2,2,256,128]{3,2,1,0:T(8,128)(2,1)} %bitcast.14), channel_id=1, source_target_pairs={{0,24},{8,0},{16,8},{24,16},{1,25},{9,1},{17,9},{25,17},{2,26},{10... | collective-permute-start | bytes 786440 | tf_op jit(solution)/shard_map/ppermute | solution.py:278
  14.3 18.7 %collective-permute-start.3 = (bf16[2,2,256,128]{3,2,1,0:T(8,128)(2,1)}, bf16[2,2,256,128]{3,2,1,0:T(8,128)(2,1)S(1)}, u32[]{:S(2)}, u32[]{:S(2)}) collective-permute-start(bf16[2,2,256,128]{3,2,1,0:T(8,128)(2,1)} %bitcast.17), channel_id=1, source_target_pairs={{0,16},{8,24},{16,0},{24,8},{1,17},{9,25},{17,1},{25,9},{2,18},{10... | collective-permute-start | bytes 786440 | tf_op jit(solution)/shard_map/ppermute | solution.py:278
  17.1 14.8 %collective-permute-start.5 = (bf16[2,2,256,128]{3,2,1,0:T(8,128)(2,1)}, bf16[2,2,256,128]{3,2,1,0:T(8,128)(2,1)}, u32[]{:S(2)}, u32[]{:S(2)}) collective-permute-start(bf16[2,2,256,128]{3,2,1,0:T(8,128)(2,1)} %bitcast.32), channel_id=1, source_target_pairs={{0,8},{8,16},{16,24},{24,0},{1,9},{9,17},{17,25},{25,1},{2,10},{10... | collective-permute-start | bytes 786440 | tf_op jit(solution)/shard_map/ppermute | solution.py:278
  18.3 14.7 %collective-permute-start.6 = (bf16[2,2,256,128]{3,2,1,0:T(8,128)(2,1)}, bf16[2,2,256,128]{3,2,1,0:T(8,128)(2,1)S(1)}, u32[]{:S(2)}, u32[]{:S(2)}) collective-permute-start(bf16[2,2,256,128]{3,2,1,0:T(8,128)(2,1)} %bitcast.35), channel_id=1, source_target_pairs={{0,24},{8,0},{16,8},{24,16},{1,25},{9,1},{17,9},{25,17},{2,26},{10... | collective-permute-start | bytes 786440 | tf_op jit(solution)/shard_map/ppermute | solution.py:278
  21.3 15.3 %collective-permute-start.7 = (bf16[2,2,256,128]{3,2,1,0:T(8,128)(2,1)S(1)}, bf16[2,2,256,128]{3,2,1,0:T(8,128)(2,1)S(1)}, u32[]{:S(2)}, u32[]{:S(2)}) collective-permute-start(bf16[2,2,256,128]{3,2,1,0:T(8,128)(2,1)S(1)} %bitcast.249), channel_id=1, source_target_pairs={{0,16},{8,24},{16,0},{24,8},{1,17},{9,25},{17,1},{25,9},{2,18},{10... | collective-permute-start | bytes 786440 | tf_op jit(solution)/shard_map/ppermute | solution.py:278
  36.8 5.6 %copy-start = (bf16[1,4,2,256,128]{4,3,2,1,0:T(8,128)(2,1)}, bf16[1,4,2,256,128]{4,3,2,1,0:T(8,128)(2,1)S(1)}, u32[]{:S(2)}) copy-start(bf16[1,4,2,256,128]{4,3,2,1,0:T(8,128)(2,1)S(1)} %get-tuple-element.120) | copy-start | bytes 1572868
  36.8 5.6 %copy-start.1 = (bf16[1,4,2,256,128]{4,3,2,1,0:T(8,128)(2,1)}, bf16[1,4,2,256,128]{4,3,2,1,0:T(8,128)(2,1)S(1)}, u32[]{:S(2)}) copy-start(bf16[1,4,2,256,128]{4,3,2,1,0:T(8,128)(2,1)S(1)} %get-tuple-element.121) | copy-start | bytes 1572868
  36.9 4.9 %collective-permute-start.8 = (bf16[2,128,128]{2,1,0:T(8,128)(2,1)S(1)}, bf16[2,128,128]{2,1,0:T(8,128)(2,1)S(1)}, u32[]{:S(2)}, u32[]{:S(2)}) collective-permute-start(bf16[2,128,128]{2,1,0:T(8,128)(2,1)S(1)} %pad_maximum_fusion.4), channel_id=1, source_target_pairs={{0,32},{32,64},{64,96},{1,33},{33,65},{65,97},{2,34},{34,66},{66,9... | collective-permute-start | bytes 196616 | tf_op jit(solution)/shard_map/ppermute | solution.py:301
  40.5 23.7 %collective-permute-start.10 = (bf16[2,128,128]{2,1,0:T(8,128)(2,1)S(1)}, bf16[2,128,128]{2,1,0:T(8,128)(2,1)S(1)}, u32[]{:S(2)}, u32[]{:S(2)}) collective-permute-start(bf16[2,128,128]{2,1,0:T(8,128)(2,1)S(1)} %pad_maximum_fusion.5), channel_id=1, source_target_pairs={{32,0},{64,32},{96,64},{33,1},{65,33},{97,65},{34,2},{66,34},{98,6... | collective-permute-start | bytes 196616 | tf_op jit(solution)/shard_map/ppermute | solution.py:305
  46.9 16.6 %collective-permute-start.12 = (bf16[2,64,128]{2,1,0:T(8,128)(2,1)S(1)}, bf16[2,64,128]{2,1,0:T(8,128)(2,1)S(1)}, u32[]{:S(2)}, u32[]{:S(2)}) collective-permute-start(bf16[2,64,128]{2,1,0:T(8,128)(2,1)S(1)} %pad_maximum_fusion.7), channel_id=1, source_target_pairs={{0,64},{32,96},{64,0},{96,32},{1,65},{33,97},{65,1},{97,33},{2,66}... | collective-permute-start | bytes 98312 | tf_op jit(solution)/shard_map/ppermute | solution.py:309
  50.9 12.6 %collective-permute-start.13 = (bf16[2,64,128]{2,1,0:T(8,128)(2,1)S(1)}, bf16[2,64,128]{2,1,0:T(8,128)(2,1)S(1)}, u32[]{:S(2)}, u32[]{:S(2)}) collective-permute-start(bf16[2,64,128]{2,1,0:T(8,128)(2,1)S(1)} %pad_maximum_fusion.7), channel_id=1, source_target_pairs={{0,96},{32,64},{64,32},{96,0},{1,97},{33,65},{65,33},{97,1},{2,98}... | collective-permute-start | bytes 98312 | tf_op jit(solution)/shard_map/ppermute | solution.py:309
  57.2 7.1 %collective-permute-start.11 = (bf16[4,2,128,128]{3,2,1,0:T(8,128)(2,1)S(1)}, bf16[4,2,128,128]{3,2,1,0:T(8,128)(2,1)S(1)}, u32[]{:S(2)}, u32[]{:S(2)}) collective-permute-start(bf16[4,2,128,128]{3,2,1,0:T(8,128)(2,1)S(1)} %get-tuple-element.150), channel_id=1, source_target_pairs={{32,0},{64,32},{96,64},{33,1},{65,33},{97,65},{34,2},{66,34},{98,6... | collective-permute-start | bytes 786440 | tf_op jit(solution)/shard_map/ppermute | solution.py:305
  58.5 7.3 %collective-permute-start.9 = (bf16[4,2,128,128]{3,2,1,0:T(8,128)(2,1)S(1)}, bf16[4,2,128,128]{3,2,1,0:T(8,128)(2,1)S(1)}, u32[]{:S(2)}, u32[]{:S(2)}) collective-permute-start(bf16[4,2,128,128]{3,2,1,0:T(8,128)(2,1)S(1)} %get-tuple-element.151), channel_id=1, source_target_pairs={{0,32},{32,64},{64,96},{1,33},{33,65},{65,97},{2,34},{34,66},{66,9... | collective-permute-start | bytes 786440 | tf_op jit(solution)/shard_map/ppermute | solution.py:301
  98.3 20.5 %collective-permute-start.18 = (bf16[5,2,128,128]{3,2,1,0:T(8,128)(2,1)}, bf16[5,2,128,128]{3,2,1,0:T(8,128)(2,1)S(1)}, u32[]{:S(2)}, u32[]{:S(2)}) collective-permute-start(bf16[5,2,128,128]{3,2,1,0:T(8,128)(2,1)} %get-tuple-element.76), channel_id=1, source_target_pairs={{0,32},{32,64},{64,96},{1,33},{33,65},{65,97},{2,34},{34,66},{66,9... | collective-permute-start | bytes 983048 | tf_op jit(solution)/shard_map/ppermute | solution.py:301
  102.1 16.7 %collective-permute-start.19 = (bf16[5,2,128,128]{3,2,1,0:T(8,128)(2,1)}, bf16[5,2,128,128]{3,2,1,0:T(8,128)(2,1)S(1)}, u32[]{:S(2)}, u32[]{:S(2)}) collective-permute-start(bf16[5,2,128,128]{3,2,1,0:T(8,128)(2,1)} %get-tuple-element.77), channel_id=1, source_target_pairs={{32,0},{64,32},{96,64},{33,1},{65,33},{97,65},{34,2},{66,34},{98,6... | collective-permute-start | bytes 983048 | tf_op jit(solution)/shard_map/ppermute | solution.py:305
  105.0 6.5 %collective-permute-start.14 = (bf16[2,2,256,128]{3,2,1,0:T(8,128)(2,1)S(1)}, bf16[2,2,256,128]{3,2,1,0:T(8,128)(2,1)S(1)}, u32[]{:S(2)}, u32[]{:S(2)}) collective-permute-start(bf16[2,2,256,128]{3,2,1,0:T(8,128)(2,1)S(1)} %get-tuple-element.118), channel_id=1, source_target_pairs={{0,8},{8,16},{16,24},{24,0},{1,9},{9,17},{17,25},{25,1},{2,10},{10... | collective-permute-start | bytes 786440 | tf_op jit(solution)/shard_map/ppermute | solution.py:291
  106.7 7.7 %collective-permute-start.15 = (bf16[2,2,256,128]{3,2,1,0:T(8,128)(2,1)S(1)}, bf16[2,2,256,128]{3,2,1,0:T(8,128)(2,1)S(1)}, u32[]{:S(2)}, u32[]{:S(2)}) collective-permute-start(bf16[2,2,256,128]{3,2,1,0:T(8,128)(2,1)S(1)} %get-tuple-element.119), channel_id=1, source_target_pairs={{0,24},{8,0},{16,8},{24,16},{1,25},{9,1},{17,9},{25,17},{2,26},{10... | collective-permute-start | bytes 786440 | tf_op jit(solution)/shard_map/ppermute | solution.py:291
  107.7 8.6 %collective-permute-start.16 = (bf16[2,2,256,128]{3,2,1,0:T(8,128)(2,1)S(1)}, bf16[2,2,256,128]{3,2,1,0:T(8,128)(2,1)S(1)}, u32[]{:S(2)}, u32[]{:S(2)}) collective-permute-start(bf16[2,2,256,128]{3,2,1,0:T(8,128)(2,1)S(1)} %get-tuple-element.116), channel_id=1, source_target_pairs={{0,16},{8,24},{16,0},{24,8},{1,17},{9,25},{17,1},{25,9},{2,18},{10... | collective-permute-start | bytes 786440 | tf_op jit(solution)/shard_map/ppermute | solution.py:291
  111.5 5.1 %collective-permute-start.20 = (bf16[2,64,128]{2,1,0:T(8,128)(2,1)S(1)}, bf16[2,64,128]{2,1,0:T(8,128)(2,1)S(1)}, u32[]{:S(2)}, u32[]{:S(2)}) collective-permute-start(bf16[2,64,128]{2,1,0:T(8,128)(2,1)S(1)} %get-tuple-element.149), channel_id=1, source_target_pairs={{0,64},{32,96},{64,0},{96,32},{1,65},{33,97},{65,1},{97,33},{2,66}... | collective-permute-start | bytes 98312 | tf_op jit(solution)/shard_map/ppermute | solution.py:309
  114.5 4.4 %collective-permute-start.21 = (bf16[2,64,128]{2,1,0:T(8,128)(2,1)S(1)}, bf16[2,64,128]{2,1,0:T(8,128)(2,1)S(1)}, u32[]{:S(2)}, u32[]{:S(2)}) collective-permute-start(bf16[2,64,128]{2,1,0:T(8,128)(2,1)S(1)} %get-tuple-element.148), channel_id=1, source_target_pairs={{0,96},{32,64},{64,32},{96,0},{1,97},{33,65},{65,33},{97,1},{2,98}... | collective-permute-start | bytes 98312 | tf_op jit(solution)/shard_map/ppermute | solution.py:309
  116.6 2.2 %copy-start.6 = (bf16[2,64,128]{2,1,0:T(8,128)(2,1)}, bf16[2,64,128]{2,1,0:T(8,128)(2,1)S(1)}, u32[]{:S(2)}) copy-start(bf16[2,64,128]{2,1,0:T(8,128)(2,1)S(1)} %collective-permute-done.20.far_a) | copy-start | bytes 98308
  118.8 0.6 copy-start.7
  118.8 0.7 copy-start.4
  118.8 0.8 copy-start.5
  126.7 13.1 %collective-permute-start.27 = (f32[2,20,128]{2,1,0:T(8,128)S(1)}, f32[2,20,128]{2,1,0:T(8,128)S(1)}, u32[]{:S(2)}, u32[]{:S(2)}) collective-permute-start(f32[2,20,128]{2,1,0:T(8,128)S(1)} %pad_maximum_fusion.8), channel_id=1, source_target_pairs={{0,32},{32,64},{64,96},{96,0},{1,33},{33,65},{65,97},{97,1},{2,34}... | collective-permute-start | bytes 61448 | tf_op jit(solution)/shard_map/ppermute | solution.py:313
  126.7 13.1 %collective-permute-start.28 = (f32[2,20,128]{2,1,0:T(8,128)S(1)}, f32[2,20,128]{2,1,0:T(8,128)S(1)}, u32[]{:S(2)}, u32[]{:S(2)}) collective-permute-start(f32[2,20,128]{2,1,0:T(8,128)S(1)} %pad_maximum_fusion.8), channel_id=1, source_target_pairs={{0,64},{32,96},{64,0},{96,32},{1,65},{33,97},{65,1},{97,33},{2,66}... | collective-permute-start | bytes 61448 | tf_op jit(solution)/shard_map/ppermute | solution.py:313
  129.5 10.3 %collective-permute-start.29 = (f32[2,20,128]{2,1,0:T(8,128)S(1)}, f32[2,20,128]{2,1,0:T(8,128)S(1)}, u32[]{:S(2)}, u32[]{:S(2)}) collective-permute-start(f32[2,20,128]{2,1,0:T(8,128)S(1)} %pad_maximum_fusion.8), channel_id=1, source_target_pairs={{0,96},{32,0},{64,32},{96,64},{1,97},{33,1},{65,33},{97,65},{2,98}... | collective-permute-start | bytes 61448 | tf_op jit(solution)/shard_map/ppermute | solution.py:313
  129.5 52.3 %collective-permute-start.17 = (bf16[4,2,256,128]{2,3,0,1:T(8,128)(2,1)S(1)}, bf16[4,2,256,128]{2,3,0,1:T(8,128)(2,1)}, u32[]{:S(2)}, u32[]{:S(2)}) collective-permute-start(bf16[4,2,256,128]{2,3,0,1:T(8,128)(2,1)S(1)} %dynamic-slice_bitcast_fusion.1), channel_id=1, source_target_pairs={{0,4},{4,0},{1,5},{5,1},{2,6},{6,2},{3,7},{7,3},{8,12},{12,8},{9,1... | collective-permute-start | bytes 1572872 | tf_op jit(solution)/shard_map/ppermute | solution.py:259
  138.4 7.1 %collective-permute-start.22 = (bf16[2,64,128]{2,1,0:T(8,128)(2,1)}, bf16[2,64,128]{2,1,0:T(8,128)(2,1)S(1)}, u32[]{:S(2)}, u32[]{:S(2)}) collective-permute-start(bf16[2,64,128]{2,1,0:T(8,128)(2,1)} %get-tuple-element.90), channel_id=1, source_target_pairs={{32,0},{64,32},{96,64},{33,1},{65,33},{97,65},{34,2},{66,34},{98,6... | collective-permute-start | bytes 98312 | tf_op jit(solution)/shard_map/ppermute | solution.py:305
  140.5 8.8 %collective-permute-start.30 = (f32[2,20,128]{2,1,0:T(8,128)S(1)}, f32[2,20,128]{2,1,0:T(8,128)S(1)}, u32[]{:S(2)}, u32[]{:S(2)}) collective-permute-start(f32[2,20,128]{2,1,0:T(8,128)S(1)} %add_add_fusion.1), channel_id=1, source_target_pairs={{0,1},{1,2},{2,3},{3,0},{4,5},{5,6},{6,7},{7,4},{8,9},{9,10},{10,1... | collective-permute-start | bytes 61448 | tf_op jit(solution)/shard_map/ppermute | solution.py:313
  141.8 10.1 %collective-permute-start.31 = (f32[2,20,128]{2,1,0:T(8,128)S(1)}, f32[2,20,128]{2,1,0:T(8,128)S(1)}, u32[]{:S(2)}, u32[]{:S(2)}) collective-permute-start(f32[2,20,128]{2,1,0:T(8,128)S(1)} %add_add_fusion.1), channel_id=1, source_target_pairs={{0,2},{1,3},{2,0},{3,1},{4,6},{5,7},{6,4},{7,5},{8,10},{9,11},{10,... | collective-permute-start | bytes 61448 | tf_op jit(solution)/shard_map/ppermute | solution.py:313
  144.5 7.5 %collective-permute-start.32 = (f32[2,20,128]{2,1,0:T(8,128)S(1)}, f32[2,20,128]{2,1,0:T(8,128)S(1)}, u32[]{:S(2)}, u32[]{:S(2)}) collective-permute-start(f32[2,20,128]{2,1,0:T(8,128)S(1)} %add_add_fusion.1), channel_id=1, source_target_pairs={{0,3},{1,0},{2,1},{3,2},{4,7},{5,4},{6,5},{7,6},{8,11},{9,8},{10,9... | collective-permute-start | bytes 61448 | tf_op jit(solution)/shard_map/ppermute | solution.py:313
  149.2 28.8 %collective-permute-start.23 = (bf16[2,2,256,128]{3,2,1,0:T(8,128)(2,1)}, bf16[2,2,256,128]{3,2,1,0:T(8,128)(2,1)}, u32[]{:S(2)}, u32[]{:S(2)}) collective-permute-start(bf16[2,2,256,128]{3,2,1,0:T(8,128)(2,1)} %get-tuple-element.112), channel_id=1, source_target_pairs={{0,8},{8,16},{16,24},{24,0},{1,9},{9,17},{17,25},{25,1},{2,10},{10... | collective-permute-start | bytes 786440 | tf_op jit(solution)/shard_map/ppermute | solution.py:291
  149.3 29.8 %collective-permute-start.24 = (bf16[2,2,256,128]{3,2,1,0:T(8,128)(2,1)}, bf16[2,2,256,128]{3,2,1,0:T(8,128)(2,1)}, u32[]{:S(2)}, u32[]{:S(2)}) collective-permute-start(bf16[2,2,256,128]{3,2,1,0:T(8,128)(2,1)} %get-tuple-element.113), channel_id=1, source_target_pairs={{0,24},{8,0},{16,8},{24,16},{1,25},{9,1},{17,9},{25,17},{2,26},{10... | collective-permute-start | bytes 786440 | tf_op jit(solution)/shard_map/ppermute | solution.py:291
  152.0 28.2 %collective-permute-start.25 = (bf16[2,2,256,128]{3,2,1,0:T(8,128)(2,1)S(1)}, bf16[2,2,256,128]{3,2,1,0:T(8,128)(2,1)}, u32[]{:S(2)}, u32[]{:S(2)}) collective-permute-start(bf16[2,2,256,128]{3,2,1,0:T(8,128)(2,1)S(1)} %get-tuple-element.110), channel_id=1, source_target_pairs={{0,16},{8,24},{16,0},{24,8},{1,17},{9,25},{17,1},{25,9},{2,18},{10... | collective-permute-start | bytes 786440 | tf_op jit(solution)/shard_map/ppermute | solution.py:291
  152.0 6.4 %collective-permute-start.33 = (f32[2,20,128]{2,1,0:T(8,128)S(1)}, f32[2,20,128]{2,1,0:T(8,128)S(1)}, u32[]{:S(2)}, u32[]{:S(2)}) collective-permute-start(f32[2,20,128]{2,1,0:T(8,128)S(1)} %add_add_fusion), channel_id=1, source_target_pairs={{0,8},{8,16},{16,24},{24,0},{1,9},{9,17},{17,25},{25,1},{2,10},{10... | collective-permute-start | bytes 61448 | tf_op jit(solution)/shard_map/ppermute | solution.py:415
  158.4 5.1 %collective-permute-start.34 = (f32[2,20,128]{2,1,0:T(8,128)S(1)}, f32[2,20,128]{2,1,0:T(8,128)S(1)}, u32[]{:S(2)}, u32[]{:S(2)}) collective-permute-start(f32[2,20,128]{2,1,0:T(8,128)S(1)} %add_add_fusion), channel_id=1, source_target_pairs={{0,16},{8,24},{16,0},{24,8},{1,17},{9,25},{17,1},{25,9},{2,18},{10... | collective-permute-start | bytes 61448 | tf_op jit(solution)/shard_map/ppermute | solution.py:415
  163.5 4.4 %collective-permute-start.35 = (f32[2,20,128]{2,1,0:T(8,128)S(1)}, f32[2,20,128]{2,1,0:T(8,128)S(1)}, u32[]{:S(2)}, u32[]{:S(2)}) collective-permute-start(f32[2,20,128]{2,1,0:T(8,128)S(1)} %add_add_fusion), channel_id=1, source_target_pairs={{0,24},{8,0},{16,8},{24,16},{1,25},{9,1},{17,9},{25,17},{2,26},{10... | collective-permute-start | bytes 61448 | tf_op jit(solution)/shard_map/ppermute | solution.py:415
  167.9 8.3 %collective-permute-start.36 = (f32[4,2,20,128]{3,1,2,0:T(2,128)S(1)}, f32[4,2,20,128]{3,1,2,0:T(2,128)S(1)}, u32[]{:S(2)}, u32[]{:S(2)}) collective-permute-start(f32[4,2,20,128]{3,1,2,0:T(2,128)S(1)} %copy_dynamic-update-slice_fusion), channel_id=1, source_target_pairs={{0,4},{4,0},{1,5},{5,1},{2,6},{6,2},{3,7},{7,3},{8,12},{12,8},{9,1... | collective-permute-start | bytes 245768 | tf_op jit(solution)/shard_map/ppermute | solution.py:259
  181.4 3.9 %collective-permute-start.26 = (bf16[4,2,256,128]{2,3,0,1:T(8,128)(2,1)S(1)}, bf16[4,2,256,128]{2,3,0,1:T(8,128)(2,1)}, u32[]{:S(2)}, u32[]{:S(2)}) collective-permute-start(bf16[4,2,256,128]{2,3,0,1:T(8,128)(2,1)S(1)} %dynamic-slice_bitcast_fusion), channel_id=1, source_target_pairs={{0,4},{4,0},{1,5},{5,1},{2,6},{6,2},{3,7},{7,3},{8,12},{12,8},{9,1... | collective-permute-start | bytes 1572872 | tf_op jit(solution)/shard_map/ppermute | solution.py:259

commit v2 on v1

v2 whole, which is shorter than its diff:
```python
import math

import jax
import jax.numpy as jnp
from jax import lax
from jax.experimental import pallas as pl
from jax.experimental.pallas import tpu as pltpu
from jax.sharding import Mesh, PartitionSpec as P


HD = 128
BLK = 128
LEVELS = 5
NZ, NX, NC, NY = 4, 4, 2, 4
ROWS = 256
GROUP = ROWS * NX * NC
PAIRS = GROUP // 256
SIZES = [GROUP >> l for l in range(LEVELS + 1)]
HALO = [64 >> l for l in range(LEVELS + 1)]
PRE = 8
OFFS = [0]
for _l in range(LEVELS):
    OFFS.append(OFFS[-1] + SIZES[_l] + 2 * BLK)
TOTAL = OFFS[LEVELS] + BLK
NBLK = TOTAL // BLK
KEYS = 4 * BLK + 8 * BLK + BLK
SCALE = HD ** -0.5
EXPC = SCALE * math.log2(math.e)
NEG = -1e30
F32 = jnp.float32
BF16 = jnp.bfloat16
SLOTS = [(0, 0), (2, 0), (2, 1), (1, 0), (3, 0), (1, 1), (3, 1), (0, 1)]
MSG = LEVELS * 2 * BLK + 2 * SIZES[LEVELS]
PARAMS = pltpu.CompilerParams(vmem_limit_bytes=24 << 20)


def nn(a, b):
    return lax.dot_general(a, b, (((1,), (0,)), ((), ())), preferred_element_type=F32)


def nt(a, b):
    return lax.dot_general(a, b, (((1,), (1,)), ((), ())), preferred_element_type=F32)


def chunks(total, step):
    return [(r, min(step, total - r)) for r in range(0, total, step)]


def peer(pos_ref, slot):
    dx, dc = SLOTS[slot]
    return ((pos_ref[1] + dx) % NX) * NC + (pos_ref[2] + dc) % NC


def source(pos_ref, slot):
    dx, dc = SLOTS[slot]
    return ((pos_ref[1] + NX - dx) % NX) * NC + (pos_ref[2] + dc) % NC


def span(index, size):
    return pl.ds(pl.multiple_of(index * size, size), size)


def msg_rows(level, side):
    if level < LEVELS:
        start = (2 * level + side) * BLK
        return slice(start, start + BLK)
    start = 2 * LEVELS * BLK + side * SIZES[LEVELS]
    return slice(start, start + SIZES[LEVELS])


def pack_kernel(pos_ref, a_ref, b_ref, *outs):
    for slot, out in enumerate(outs):
        lanes = span(peer(pos_ref, slot), HD)
        out[0] = a_ref[0, :, lanes]
        out[1] = b_ref[0, :, lanes]


def unpack_kernel(pos_ref, *refs):
    slots, (a_ref, b_ref) = refs[:-2], refs[-2:]
    for slot, ref in enumerate(slots):
        lanes = span(source(pos_ref, slot), HD)
        a_ref[0, :, lanes] = ref[0]
        b_ref[0, :, lanes] = ref[1]


def back_pack_kernel(pos_ref, fine_ref, halo_ref, *outs):
    for slot, out in enumerate(outs):
        p = peer(pos_ref, slot)
        last = (p == NX * NC - 1).astype(F32)
        edge = ROWS - HALO[0]
        for side in range(2):
            out[side, 0:edge] = fine_ref[side, pl.ds(pl.multiple_of(p * ROWS, ROWS), edge), :]
            tail = fine_ref[side, pl.ds(pl.multiple_of(p * ROWS + edge, HALO[0]), HALO[0]), :]
            out[side, edge:ROWS] = (tail.astype(F32) + halo_ref[side].astype(F32) * last).astype(BF16)


def weights_kernel(pos_ref, *refs):
    slots, outs = refs[:-2], refs[-2:]
    for slot, ref in enumerate(slots):
        lanes = span(source(pos_ref, slot), HD)
        for side in range(2):
            for level in range(LEVELS):
                row = side * 4 * LEVELS + 4 * level
                outs[side][level, :, lanes] = ref[row : row + 4, :]


def coarse_kernel(pos_ref, halo_ref, wk_ref, wv_ref, *refs):
    pieces, outs = refs[: len(SLOTS)], refs[len(SLOTS) :]
    wides = (outs[0:LEVELS], outs[LEVELS : 2 * LEVELS])
    exts = outs[2 * LEVELS : 2 * LEVELS + 2]
    up_ref, down_ref, last_ref = outs[2 * LEVELS + 2 :]
    lanes = span(pos_ref[1] * NC + pos_ref[2], HD)
    for side in range(2):
        weight, wide, ext = (wk_ref, wv_ref)[side], wides[side], exts[side]
        x = wide[0]
        x[0:PRE, :] = jnp.zeros((PRE, HD), F32)
        x[PRE : PRE + HALO[0], :] = halo_ref[side].astype(F32)
        for slot, piece in enumerate(pieces):
            start = source(pos_ref, slot) * ROWS
            value = piece[side]
            x[pl.ds(pl.multiple_of(PRE + HALO[0] + start, 8), ROWS), :] = value.astype(F32)
            ext[pl.ds(pl.multiple_of(BLK + start, BLK), ROWS), :] = value
        for level in range(1, LEVELS + 1):
            x = wide[level - 1]
            taps = [weight[level - 1, j : j + 1, lanes] for j in range(4)]
            if level < LEVELS:
                wide[level][0:PRE, :] = jnp.zeros((PRE, HD), F32)
            first = 0 if level < LEVELS else HALO[level]
            for r, n in chunks(HALO[level] + SIZES[level] - first, 128):
                r += first
                acc = None
                for j in range(4):
                    term = taps[j] * x[pl.ds(PRE + 2 * r - 2 + j, n, stride=2), :]
                    acc = term if acc is None else acc + term
                low = acc.astype(BF16)
                if level < LEVELS:
                    wide[level][PRE + r : PRE + r + n, :] = low.astype(F32)
                else:
                    for ref in (up_ref, down_ref):
                        ref[msg_rows(LEVELS, side), :] = low
                    last_ref[side * n : (side + 1) * n, :] = low
            if level < LEVELS:
                for r, n in chunks(SIZES[level], 256):
                    start = PRE + HALO[level] + r
                    to = OFFS[level] + BLK + r
                    ext[to : to + n, :] = wide[level][start : start + n, :].astype(BF16)
        for level in range(LEVELS):
            begin = OFFS[level] + BLK
            end = begin + SIZES[level]
            down_ref[msg_rows(level, side), :] = ext[begin : begin + BLK, :]
            up_ref[msg_rows(level, side), :] = ext[end - BLK : end, :]


def attention_kernel(pos_ref, *refs):
    n = len(SLOTS)
    pieces = refs[:n]
    k_in, v_in, from_below, from_above, far_ref = refs[n : n + 5]
    sends = refs[n + 5 : 2 * n + 5]
    up_ref, down_ref, gfar_ref, dk_ref, dv_ref = refs[2 * n + 5 : 2 * n + 10]
    kx, vx, kt, vt, s_ref, e_ref, q_ref, do_ref, att_ref, dq_ref = refs[2 * n + 10 :]
    z = pos_ref[0]
    half = SIZES[LEVELS]
    far = OFFS[LEVELS]
    even = z % 2 == 0
    for slot, piece in enumerate(pieces):
        rows = span(source(pos_ref, slot), ROWS)
        q_ref[rows, :] = piece[0]
        do_ref[rows, :] = piece[1]
    for side, (own, ext, tr, grad) in enumerate(((k_in, kx, kt, dk_ref), (v_in, vx, vt, dv_ref))):
        for level in range(LEVELS):
            begin = OFFS[level] + BLK
            end = begin + SIZES[level]
            ext[begin - BLK : begin, :] = from_below[msg_rows(level, side), :]
            for r, m in chunks(SIZES[level], 256):
                ext[begin + r : begin + r + m, :] = own[begin + r : begin + r + m, :]
            ext[end : end + BLK, :] = from_above[msg_rows(level, side), :]
        ext[far : far + half, :] = far_ref[side * half : (side + 1) * half, :]
        rows = msg_rows(LEVELS, side)
        ext[far + half : far + 2 * half, :] = jnp.where(even, from_below[rows, :], from_above[rows, :])

        def prepare(i, _, ext=ext, tr=tr, grad=grad):
            rows = span(i, BLK)
            tr[i] = ext[rows, :].T
            grad[rows, :] = jnp.zeros((BLK, HD), F32)
            return 0

        lax.fori_loop(0, NBLK, prepare, 0)

    lane = lax.broadcasted_iota(jnp.int32, (BLK, 2 * BLK), 1)

    def pair(p, _):
        qrows = pl.ds(pl.multiple_of(p * 256, 256), 256)
        qt = q_ref[qrows, :].T
        dot_t = do_ref[qrows, :].astype(F32).T
        groups = [[2 * p + i for i in range(4)]]
        valid = [None]
        for level in range(1, LEVELS):
            c = p >> (level - 1)
            base = OFFS[level] // BLK
            groups.append([base + c, base + c + 2])
            count = SIZES[level] // BLK
            valid.append((jnp.logical_or(c > 0, z > 0), jnp.logical_or(c < count - 1, z < NZ - 1)))
        groups.append([OFFS[LEVELS] // BLK])
        valid.append((None,))

        def rows_of(ext, blocks, contiguous):
            if contiguous:
                return ext[pl.ds(pl.multiple_of(blocks[0] * BLK, BLK), BLK * len(blocks)), :]
            parts = [ext[pl.ds(pl.multiple_of(b * BLK, BLK), BLK), :] for b in blocks]
            return parts[0] if len(parts) == 1 else jnp.concatenate(parts, 0)

        def cols_of(tr, blocks):
            parts = [tr[b] for b in blocks]
            return parts[0] if len(parts) == 1 else jnp.concatenate(parts, 1)

        top = jnp.full((8, 256), NEG, F32)
        row = 0
        for gid, blocks in enumerate(groups):
            n = BLK * len(blocks)
            s = nn(rows_of(kx, blocks, gid == 0), qt)
            for i in range(len(blocks)):
                part = s[i * BLK : (i + 1) * BLK, :]
                if gid == 0 and i == 0:
                    lim = jnp.where(jnp.logical_or(p > 0, z > 0), BLK, 0)
                    part = jnp.where(lane < lim, part, NEG)
                elif gid == 0 and i == 3:
                    lim = jnp.where(jnp.logical_or(p < PAIRS - 1, z < NZ - 1), BLK, 2 * BLK)
                    part = jnp.where(lane >= lim, part, NEG)
                elif gid > 0 and valid[gid][i] is not None:
                    part = jnp.where(valid[gid][i], part, NEG)
                s_ref[row + i * BLK : row + (i + 1) * BLK, :] = part
                top = jnp.maximum(top, jnp.max(part.reshape(BLK // 8, 8, 256), 0))
            row += n
        shift = jnp.max(top, 0, keepdims=True) * EXPC
        total = jnp.zeros((8, 256), F32)
        out_t = jnp.zeros((HD, 256), F32)
        row = 0
        for blocks in groups:
            n = BLK * len(blocks)
            e = jnp.exp2(s_ref[row : row + n, :] * EXPC - shift)
            total = total + jnp.sum(e.reshape(n // 8, 8, 256), 0)
            low = e.astype(BF16)
            e_ref[row : row + n, :] = low
            out_t = out_t + nn(cols_of(vt, blocks), low)
            row += n
        inverse = 1.0 / jnp.sum(total, 0, keepdims=True)
        out_t = out_t * inverse
        att_ref[qrows, :] = out_t.T.astype(BF16)
        don_t = (dot_t * inverse).astype(BF16)
        delta = jnp.sum(don_t.astype(F32) * out_t, 0, keepdims=True)
        dq_t = jnp.zeros((HD, 256), F32)
        row = 0
        for gid, blocks in enumerate(groups):
            n = BLK * len(blocks)
            low = e_ref[row : row + n, :]
            dp = nn(rows_of(vx, blocks, gid == 0), don_t)
            ds = (low.astype(F32) * (dp - delta)).astype(BF16)
            dq_t = dq_t + nn(cols_of(kt, blocks), ds)
            dk = nt(ds, qt)
            dv = nt(low, don_t)
            for i, b in enumerate(blocks):
                rows = pl.ds(pl.multiple_of(b * BLK, BLK), BLK)
                dk_ref[rows, :] += dk[i * BLK : (i + 1) * BLK, :]
                dv_ref[rows, :] += dv[i * BLK : (i + 1) * BLK, :]
            row += n
        dq_ref[qrows, :] = (dq_t * SCALE).T.astype(BF16)
        return 0

    lax.fori_loop(0, PAIRS, pair, 0)
    for side, (grad, mult) in enumerate(((dk_ref, SCALE), (dv_ref, 1.0))):
        for level in range(LEVELS):
            begin = OFFS[level] + BLK
            end = begin + SIZES[level]
            down_ref[msg_rows(level, side), :] = (grad[begin - BLK : begin, :] * mult).astype(BF16)
            up_ref[msg_rows(level, side), :] = (grad[end : end + BLK, :] * mult).astype(BF16)
        gfar_ref[side * half : (side + 1) * half, :] = (grad[far : far + half, :] * mult).astype(BF16)
        other = (grad[far + half : far + 2 * half, :] * mult).astype(BF16)
        for ref in (up_ref, down_ref):
            ref[msg_rows(LEVELS, side), :] = other
    for slot, send in enumerate(sends):
        rows = span(peer(pos_ref, slot), ROWS)
        send[0] = att_ref[rows, :]
        send[1] = dq_ref[rows, :]


def back_kernel(pos_ref, dk_ref, dv_ref, from_left, from_right, far_ref, wk_ref, wv_ref, *refs):
    xs = (refs[0:LEVELS], refs[LEVELS : 2 * LEVELS])
    fine_out, halo_out, gw_out = refs[2 * LEVELS : 2 * LEVELS + 3]
    g = refs[2 * LEVELS + 3 :]
    half = SIZES[LEVELS]
    even = pos_ref[0] % 2 == 0
    lanes = span(pos_ref[1] * NC + pos_ref[2], HD)
    for side in range(2):
        weight = (wk_ref, wv_ref)[side]
        grad = (dk_ref, dv_ref)[side]
        mult = (SCALE, 1.0)[side]
        base = side * 4 * LEVELS
        end = HALO[LEVELS] + SIZES[LEVELS]
        g[LEVELS][0 : HALO[LEVELS], :] = jnp.zeros((HALO[LEVELS], HD), F32)
        g[LEVELS][HALO[LEVELS] : end, :] = (
            far_ref[side * half : (side + 1) * half, :].astype(F32)
            + jnp.where(even, from_left[msg_rows(LEVELS, side), :], from_right[msg_rows(LEVELS, side), :]).astype(F32)
        )
        g[LEVELS][end : end + 8, :] = jnp.zeros((8, HD), F32)
        for level in range(LEVELS, 0, -1):
            taps = [weight[level - 1, j : j + 1, lanes] for j in range(4)]
            x = xs[side][level - 1]
            here, below = g[level], g[level - 1]
            sums = [jnp.zeros((8, HD), F32) for _ in range(4)]
            total = HALO[level] + SIZES[level]
            for r, n in chunks(total, 128):
                g0 = here[r : r + n, :]
                g1 = here[r + 1 : r + n + 1, :]
                below[pl.ds(2 * r, n, stride=2), :] = taps[2] * g0 + taps[0] * g1
                below[pl.ds(2 * r + 1, n, stride=2), :] = taps[3] * g0 + taps[1] * g1
                for j in range(4):
                    prod = g0 * x[pl.ds(PRE + 2 * r - 2 + j, n, stride=2), :]
                    if n % 8 == 0:
                        sums[j] = sums[j] + jnp.sum(prod.reshape(n // 8, 8, HD), 0)
                    else:
                        gap = jnp.zeros((8 - n % 8, HD), F32)
                        prod = jnp.concatenate([prod, gap], 0)
                        sums[j] = sums[j] + jnp.sum(prod.reshape((n + 7) // 8, 8, HD), 0)
            for j in range(4):
                row = base + 4 * (level - 1) + j
                gw_out[row : row + 1, :] = jnp.sum(sums[j], 0, keepdims=True)
            low = level - 1
            off = OFFS[low] + BLK
            size, pad = SIZES[low], HALO[low]
            for r, n in chunks(size, 128):
                value = below[pad + r : pad + r + n, :] + grad[off + r : off + r + n, :] * mult
                if r == 0:
                    value = value + from_left[msg_rows(low, side), :].astype(F32)
                if r == size - BLK:
                    value = value + from_right[msg_rows(low, side), :].astype(F32)
                if low > 0:
                    below[pad + r : pad + r + n, :] = value
                else:
                    fine_out[side, r : r + n, :] = value.astype(BF16)
            if low > 0:
                below[pad + size : pad + size + 8, :] = jnp.zeros((8, HD), F32)
            else:
                halo_out[side] = below[0:pad, :].astype(BF16)


def exchange(slots):
    received = [slots[0]]
    for i, (dx, dc) in enumerate(SLOTS[1:], 1):
        pairs = [(x * NC + c, (x + dx) % NX * NC + (c + dc) % NC) for x in range(NX) for c in range(NC)]
        received.append(lax.ppermute(slots[i], ("x", "c"), pairs))
    return received


def ring(value, axis, k, size=4):
    return lax.ppermute(value, axis, [(i, (i + k) % size) for i in range(size)])


def across(value, flip):
    return lax.ppermute(value, "z", [(i, i ^ flip) for i in range(NZ)])


def sum_over(value, axis):
    return value + sum(ring(value, axis, k) for k in (1, 2, 3))


def smem():
    return pl.BlockSpec(memory_space=pltpu.SMEM)


def vmem():
    return pl.BlockSpec(memory_space=pltpu.VMEM)


def sds(shape, dtype):
    return jax.ShapeDtypeStruct(shape, dtype)


def call(kernel, out_shape, pos, *args, scratch=()):
    return pl.pallas_call(
        kernel,
        out_shape=out_shape,
        in_specs=[smem()] + [vmem()] * len(args),
        out_specs=[vmem()] * len(out_shape),
        scratch_shapes=list(scratch),
        compiler_params=PARAMS,
    )(pos, *args)


def layer(queries, key_rows, value_rows, conv_key, conv_value, grad_out):
    z, x, c = lax.axis_index("z"), lax.axis_index("x"), lax.axis_index("c")
    pos = jnp.stack([z, x, c]).astype(jnp.int32)
    slot_shape = [sds((2, ROWS, HD), BF16)] * len(SLOTS)
    row_shape = [sds((1, ROWS, NX * NC * HD), BF16)] * 2
    msg = sds((MSG, HD), BF16)
    far_shape = sds((2 * SIZES[LEVELS], HD), BF16)
    ext_shape = sds((TOTAL, HD), BF16)
    ext_grad = sds((TOTAL, HD), F32)

    kv = exchange(call(pack_kernel, slot_shape, pos, key_rows, value_rows))
    halo = jnp.zeros((2, HALO[0], HD), BF16)
    for (dx, dc), piece in zip(SLOTS, kv):
        here = jnp.logical_and((x + 1) % NX == dx, (c + dc) % NC == 1)
        halo = jnp.where(here, piece[:, ROWS - HALO[0] :], halo)
    qd = call(pack_kernel, slot_shape, pos, queries, grad_out)
    halo, *qd = lax.optimization_barrier((halo, *qd))
    halo = lax.ppermute(halo, "z", [(i, i + 1) for i in range(NZ - 1)])
    qd = exchange(qd)

    wides = [sds((PRE + HALO[l] + SIZES[l], HD), F32) for l in range(LEVELS)] * 2
    made = call(
        coarse_kernel, wides + [ext_shape, ext_shape, msg, msg, far_shape], pos, halo, conv_key, conv_value, *kv
    )
    wides, (k_ext, v_ext, up, down, last) = made[: 2 * LEVELS], made[2 * LEVELS :]
    from_below, from_above = ring(up, "z", 1), ring(down, "z", 3)
    far = across(last, 2)

    scratch = [
        pltpu.VMEM((TOTAL, HD), BF16),
        pltpu.VMEM((TOTAL, HD), BF16),
        pltpu.VMEM((NBLK, HD, BLK), BF16),
        pltpu.VMEM((NBLK, HD, BLK), BF16),
        pltpu.VMEM((KEYS, 256), F32),
        pltpu.VMEM((KEYS, 256), BF16),
    ] + [pltpu.VMEM((GROUP, HD), BF16)] * 4
    made = call(
        attention_kernel, slot_shape + [msg, msg, far_shape, ext_grad, ext_grad],
        pos, *qd, k_ext, v_ext, from_below, from_above, far, scratch=scratch,
    )
    sends, (up, down, far, dk, dv) = made[: len(SLOTS)], made[len(SLOTS) :]
    from_left, from_right = ring(up, "z", 1), ring(down, "z", 3)
    far = across(far, 2)
    attended, grad_query = call(unpack_kernel, row_shape, pos, *exchange(sends))

    fine, halo, gw = call(
        back_kernel,
        [sds((2, GROUP, HD), BF16), sds((2, HALO[0], HD), BF16), sds((8 * LEVELS, HD), F32)],
        pos, dk, dv, from_left, from_right, far, conv_key, conv_value, *wides,
        scratch=[pltpu.VMEM((HALO[l] + SIZES[l] + 8, HD), F32) for l in range(LEVELS + 1)],
    )
    halo = lax.ppermute(halo, "z", [(i + 1, i) for i in range(NZ - 1)])
    sends = call(back_pack_kernel, slot_shape, pos, fine, halo)
    grad_key, grad_value = call(unpack_kernel, row_shape, pos, *exchange(sends))

    gw = sum_over(sum_over(gw, "z"), "y")
    weight_shape = [sds((LEVELS, 4, NX * NC * HD), F32)] * 2
    grad_ck, grad_cv = call(weights_kernel, weight_shape, pos, *exchange([gw] * len(SLOTS)))
    return attended, grad_query, grad_key, grad_value, grad_ck, grad_cv


def solution(mesh):
    split = Mesh(mesh.devices.reshape(NZ, NX, NC, NY), ("z", "x", "c", "y"))
    rows = P("y", ("z", "x", "c"), None)
    return jax.shard_map(
        layer,
        mesh=split,
        in_specs=(rows, rows, rows, P(), P(), rows),
        out_specs=(rows, rows, rows, rows, P(), P()),
        check_vma=False,
    )
```

time: 190 us -> 150 us (0.79)
  local copies, waits for them, and re-layouts: 30.8 us -> 2.1 us
  other arithmetic: 14.8 us -> 0.11 us
  starting transfers between devices: 72.6 us -> 85.5 us
  waiting for transfers between devices: 27.3 us -> 21.9 us
  Pallas kernels: 41.8 us -> 39.1 us
    ppermute x33 -> x47, starting transfers between devices: 63.4 us -> 84.3 us  [the longest x35 64.5 us: exchange(): received.append(lax.ppermute(slots[i], ('x', 'c'), pairs))]
    ppermute x33 -> x47, waiting for transfers between devices: 25.1 us -> 12.7 us  [the longest x35 11 us: exchange(): received.append(lax.ppermute(slots[i], ('x', 'c'), pairs))]
    ppermute x4 -> x2, starting transfers between devices: 9.21 us -> 1.28 us  [across(): return lax.ppermute(value, 'z', [(i, i ^ flip) for i in range(NZ)])]
    ppermute x4 -> x2, waiting for transfers between devices: 2.19 us -> 9.15 us  [across(): return lax.ppermute(value, 'z', [(i, i ^ flip) for i in range(NZ)])]
    unnamed x24 -> x12, local copies, waits for them, and re-layouts: 7.83 us -> 2.1 us
    dynamic_slice x9 -> x0, local copies, waits for them, and re-layouts: 5.39 us -> none  [the longest x8 4.67 us: take(): return lax.dynamic_index_in_dim(value, index, dim, keepdims=False)]
    another operation x12 -> x0, local copies, waits for them, and re-layouts: 5.27 us -> none  [the longest x6 4.68 us: per_device(): jnp.stack([own_k[i][:BLK], own_v[i][:BLK]], 0)]
    squeeze x4 -> x0, other arithmetic: 5.25 us -> none  [take(): return lax.dynamic_index_in_dim(value, index, dim, keepdims=False)]
  transfers between devices with their start and end apart: 37 -> 49, of which waited for: 10 -> 10; matrix products, arithmetic and copies ran while one was open for 19% -> 0% of each run, Pallas kernels for 2% -> 4%
where the time goes in v2:
time: 150 us
  starting transfers between devices  85.5 us (57%)
  Pallas kernels  39.1 us (26%)
  waiting for transfers between devices  21.9 us (15%)
  local copies, waits for them, and re-layouts  2.1 us (1%)
    ppermute x35, starting transfers between devices, exchange(): received.append(lax.ppermute(slots[i], ('x', 'c'), pairs))  64.5 us
    pallas_call x9, Pallas kernels, call(): pl.pallas_call(kernel, out_shape=out_shape, in_specs=[smem()] + [vmem()]...  39.1 us
    ppermute x10, starting transfers between devices, ring(): return lax.ppermute(value, axis, [(i, (i + k) % size) for i in range(size)])  14.9 us
    ppermute x35, waiting for transfers between devices, exchange(): received.append(lax.ppermute(slots[i], ('x', 'c'), pairs))  11 us
    ppermute x2, waiting for transfers between devices, across(): return lax.ppermute(value, 'z', [(i, i ^ flip) for i in range(NZ)])  9.15 us
    ppermute x1, starting transfers between devices, layer(): halo = lax.ppermute(halo, 'z', [(i, i + 1) for i in range(NZ - 1)])  3.54 us
  transfers between devices with their start and end apart: 49, of which 10 were waited for; matrix products, arithmetic and copies ran while one was open for 0% of the time, Pallas kernels for 4%

profile of v2, /device:TPU:1, one launch (start us, length us, event | category | flops | bytes accessed | tf_op | source)
XLA Modules:
  0.0 149.5 jit_solution(11803336521673334955)
XLA Ops:
  0.7 1.0 copy-done
  1.8 1.0 copy-done.1
  2.8 0.8 shard_map.109
  3.7 1.5 collective-permute-start
  5.1 2.6 %collective-permute-start.1 = (bf16[2,256,128]{2,1,0:T(8,128)(2,1)S(1)}, bf16[2,256,128]{2,1,0:T(8,128)(2,1)S(1)}, u32[]{:S(2)}, u32[]{:S(2)}) collective-permute-start(bf16[2,256,128]{2,1,0:T(8,128)(2,1)S(1)} %get-tuple-element.77), channel_id=1, source_target_pairs={{0,28},{4,24},{8,4},{12,0},{16,12},{20,8},{24,20},{28,16},{1,29},{... | collective-permute-start | bytes 393224 | tf_op jit(solution)/shard_map/ppermute | solution.py:350
  7.7 3.0 %collective-permute-start.3 = (bf16[2,256,128]{2,1,0:T(8,128)(2,1)S(1)}, bf16[2,256,128]{2,1,0:T(8,128)(2,1)S(1)}, u32[]{:S(2)}, u32[]{:S(2)}) collective-permute-start(bf16[2,256,128]{2,1,0:T(8,128)(2,1)S(1)} %get-tuple-element.79), channel_id=1, source_target_pairs={{0,24},{4,28},{8,0},{12,4},{16,8},{20,12},{24,16},{28,20},{1,25},{... | collective-permute-start | bytes 393224 | tf_op jit(solution)/shard_map/ppermute | solution.py:350
  10.7 1.4 collective-permute-start.5
  12.1 1.8 %collective-permute-start.6 = (bf16[2,256,128]{2,1,0:T(8,128)(2,1)S(1)}, bf16[2,256,128]{2,1,0:T(8,128)(2,1)S(1)}, u32[]{:S(2)}, u32[]{:S(2)}) collective-permute-start(bf16[2,256,128]{2,1,0:T(8,128)(2,1)S(1)} %get-tuple-element.82), channel_id=1, source_target_pairs={{0,16},{4,20},{8,24},{12,28},{16,0},{20,4},{24,8},{28,12},{1,17},{... | collective-permute-start | bytes 393224 | tf_op jit(solution)/shard_map/ppermute | solution.py:350
  13.9 0.8 shard_map.110
  14.8 7.7 %collective-permute-done.4.refs_3_ = bf16[2,256,128]{2,1,0:T(8,128)(2,1)S(1)} collective-permute-done((bf16[2,256,128]{2,1,0:T(8,128)(2,1)S(1)}, bf16[2,256,128]{2,1,0:T(8,128)(2,1)S(1)}, u32[]{:S(2)}, u32[]{:S(2)}) %collective-permute-start.4) | collective-permute-done | bytes 131104 | tf_op jit(solution)/shard_map/ppermute | solution.py:350
  22.5 3.5 %collective-permute-start.14 = (bf16[2,64,128]{2,1,0:T(8,128)(2,1)S(1)}, bf16[2,64,128]{2,1,0:T(8,128)(2,1)S(1)}, u32[]{:S(2)}, u32[]{:S(2)}) collective-permute-start(bf16[2,64,128]{2,1,0:T(8,128)(2,1)S(1)} %fusion.5), channel_id=1, source_target_pairs={{0,32},{32,64},{64,96},{1,33},{33,65},{65,97},{2,34},{34,66},{66,9... | collective-permute-start | bytes 98312 | tf_op jit(solution)/shard_map/ppermute | solution.py:406
  27.0 1.6 %shard_map.111 = (f32[2120,128]{1,0:T(8,128)S(1)}, f32[1064,128]{1,0:T(8,128)S(1)}, f32[536,128]{1,0:T(8,128)S(1)}, f32[272,128]{1,0:T(8,128)S(1)}, f32[140,128]...) custom-call(s32[3]{0:T(128)S(1)} %pad_add_fusion.pos_ref, ...), custom_call_target="tpu_custom_call" | custom-call | tf_op jit(solution)/shard_map/pallas_call | solution.py:379
  28.7 1.8 %collective-permute-start.15 = (bf16[1408,128]{1,0:T(8,128)(2,1)S(1)}, bf16[1408,128]{1,0:T(8,128)(2,1)S(1)}, u32[]{:S(2)}, u32[]{:S(2)}) collective-permute-start(bf16[1408,128]{1,0:T(8,128)(2,1)S(1)} %get-tuple-element.103), channel_id=1, source_target_pairs={{0,32},{32,64},{64,96},{96,0},{1,33},{33,65},{65,97},{97,1},{2,34}... | collective-permute-start | bytes 1081352 | tf_op jit(solution)/shard_map/ppermute | solution.py:355
  30.5 2.2 %collective-permute-start.16 = (bf16[1408,128]{1,0:T(8,128)(2,1)S(1)}, bf16[1408,128]{1,0:T(8,128)(2,1)S(1)}, u32[]{:S(2)}, u32[]{:S(2)}) collective-permute-start(bf16[1408,128]{1,0:T(8,128)(2,1)S(1)} %get-tuple-element.104), channel_id=1, source_target_pairs={{0,96},{32,0},{64,32},{96,64},{1,97},{33,1},{65,33},{97,65},{2,98}... | collective-permute-start | bytes 1081352 | tf_op jit(solution)/shard_map/ppermute | solution.py:355
  32.7 1.2 collective-permute-start.17
  33.9 4.0 %collective-permute-start.8 = (bf16[2,256,128]{2,1,0:T(8,128)(2,1)S(1)}, bf16[2,256,128]{2,1,0:T(8,128)(2,1)S(1)}, u32[]{:S(2)}, u32[]{:S(2)}) collective-permute-start(bf16[2,256,128]{2,1,0:T(8,128)(2,1)S(1)} %get-tuple-element.94), channel_id=1, source_target_pairs={{0,20},{4,16},{8,28},{12,24},{16,4},{20,0},{24,12},{28,8},{1,21},{... | collective-permute-start | bytes 393224 | tf_op jit(solution)/shard_map/ppermute | solution.py:350
  38.0 2.5 %collective-permute-done.17.refs_12_ = bf16[128,128]{1,0:T(8,128)(2,1)S(1)} collective-permute-done((bf16[128,128]{1,0:T(8,128)(2,1)S(1)}, bf16[128,128]{1,0:T(8,128)(2,1)S(1)}, u32[]{:S(2)}, u32[]{:S(2)}) %collective-permute-start.17) | collective-permute-done | bytes 32800 | tf_op jit(solution)/shard_map/ppermute | solution.py:359
  40.5 2.7 %collective-permute-start.10 = (bf16[2,256,128]{2,1,0:T(8,128)(2,1)S(1)}, bf16[2,256,128]{2,1,0:T(8,128)(2,1)S(1)}, u32[]{:S(2)}, u32[]{:S(2)}) collective-permute-start(bf16[2,256,128]{2,1,0:T(8,128)(2,1)S(1)} %get-tuple-element.96), channel_id=1, source_target_pairs={{0,24},{4,28},{8,0},{12,4},{16,8},{20,12},{24,16},{28,20},{1,25},{... | collective-permute-start | bytes 393224 | tf_op jit(solution)/shard_map/ppermute | solution.py:350
  43.1 2.3 %collective-permute-start.11 = (bf16[2,256,128]{2,1,0:T(8,128)(2,1)S(1)}, bf16[2,256,128]{2,1,0:T(8,128)(2,1)S(1)}, u32[]{:S(2)}, u32[]{:S(2)}) collective-permute-start(bf16[2,256,128]{2,1,0:T(8,128)(2,1)S(1)} %get-tuple-element.97), channel_id=1, source_target_pairs={{0,12},{4,8},{8,20},{12,16},{16,28},{20,24},{24,4},{28,0},{1,13},{... | collective-permute-start | bytes 393224 | tf_op jit(solution)/shard_map/ppermute | solution.py:350
  45.5 4.4 %collective-permute-start.12 = (bf16[2,256,128]{2,1,0:T(8,128)(2,1)S(1)}, bf16[2,256,128]{2,1,0:T(8,128)(2,1)S(1)}, u32[]{:S(2)}, u32[]{:S(2)}) collective-permute-start(bf16[2,256,128]{2,1,0:T(8,128)(2,1)S(1)} %get-tuple-element.98), channel_id=1, source_target_pairs={{0,28},{4,24},{8,4},{12,0},{16,12},{20,8},{24,20},{28,16},{1,29},{... | collective-permute-start | bytes 393224 | tf_op jit(solution)/shard_map/ppermute | solution.py:350
  50.1 1.1 collective-permute-done.11.refs_5_
  51.2 1.7 %collective-permute-done.12.refs_6_ = bf16[2,256,128]{2,1,0:T(8,128)(2,1)S(1)} collective-permute-done((bf16[2,256,128]{2,1,0:T(8,128)(2,1)S(1)}, bf16[2,256,128]{2,1,0:T(8,128)(2,1)S(1)}, u32[]{:S(2)}, u32[]{:S(2)}) %collective-permute-start.12) | collective-permute-done | bytes 131104 | tf_op jit(solution)/shard_map/ppermute | solution.py:350
  52.9 27.7 %shard_map.112 = (bf16[2,256,128]{2,1,0:T(8,128)(2,1)S(1)}, bf16[2,256,128]{2,1,0:T(8,128)(2,1)S(1)}, bf16[2,256,128]{2,1,0:T(8,128)(2,1)S(1)}, bf16[2,256,128]{...) custom-call(s32[3]{0:T(128)S(1)} %pad_add_fusion.pos_ref, ...), custom_call_target="tpu_custom_call" | custom-call | tf_op jit(solution)/shard_map/pallas_call | solution.py:379
  80.7 0.9 collective-permute-start.25
  81.6 1.8 %collective-permute-start.26 = (bf16[1408,128]{1,0:T(8,128)(2,1)S(1)}, bf16[1408,128]{1,0:T(8,128)(2,1)S(1)}, u32[]{:S(2)}, u32[]{:S(2)}) collective-permute-start(bf16[1408,128]{1,0:T(8,128)(2,1)S(1)} %get-tuple-element.119), channel_id=1, source_target_pairs={{0,96},{32,0},{64,32},{96,64},{1,97},{33,1},{65,33},{97,65},{2,98}... | collective-permute-start | bytes 1081352 | tf_op jit(solution)/shard_map/ppermute | solution.py:355
  83.5 6.6 %collective-permute-done.27.far_ref = bf16[128,128]{1,0:T(8,128)(2,1)S(1)} collective-permute-done((bf16[128,128]{1,0:T(8,128)(2,1)S(1)}, bf16[128,128]{1,0:T(8,128)(2,1)S(1)}, u32[]{:S(2)}, u32[]{:S(2)}) %collective-permute-start.27) | collective-permute-done | bytes 32800 | tf_op jit(solution)/shard_map/ppermute | solution.py:359
  90.7 2.5 %shard_map.114 = (bf16[2,2048,128]{2,1,0:T(8,128)(2,1)S(1)}, bf16[2,64,128]{2,1,0:T(8,128)(2,1)S(1)}, f32[40,128]{1,0:T(8,128)S(1)}) custom-call(s32[3]{0:T(128)S(1)} %pad_add_fusion.pos_ref, f32[5376,128]{1,0:T(8,128)S(1)} %get-tuple-element.116.dk_ref, f32[5376,128]{1,0:T(8,128)S(1)} %get-tuple-element.117.dv_ref, ...), custom_call_target="tpu_custom_call" | custom-call | tf_op jit(solution)/shard_map/pallas_call | solution.py:379
  93.2 2.5 %collective-permute-start.38 = (f32[40,128]{1,0:T(8,128)S(1)}, f32[40,128]{1,0:T(8,128)S(1)}, u32[]{:S(2)}, u32[]{:S(2)}) collective-permute-start(f32[40,128]{1,0:T(8,128)S(1)} %get-tuple-element.143), channel_id=1, source_target_pairs={{0,96},{32,0},{64,32},{96,64},{1,97},{33,1},{65,33},{97,65},{2,98}... | collective-permute-start | bytes 61448 | tf_op jit(solution)/shard_map/ppermute | solution.py:355
  96.4 3.1 %collective-permute-start.18 = (bf16[2,256,128]{2,1,0:T(8,128)(2,1)S(1)}, bf16[2,256,128]{2,1,0:T(8,128)(2,1)S(1)}, u32[]{:S(2)}, u32[]{:S(2)}) collective-permute-start(bf16[2,256,128]{2,1,0:T(8,128)(2,1)S(1)} %get-tuple-element.107), channel_id=1, source_target_pairs={{0,16},{4,20},{8,24},{12,28},{16,0},{20,4},{24,8},{28,12},{1,17},{... | collective-permute-start | bytes 393224 | tf_op jit(solution)/shard_map/ppermute | solution.py:350
  99.5 3.6 %collective-permute-start.19 = (bf16[2,256,128]{2,1,0:T(8,128)(2,1)S(1)}, bf16[2,256,128]{2,1,0:T(8,128)(2,1)S(1)}, u32[]{:S(2)}, u32[]{:S(2)}) collective-permute-start(bf16[2,256,128]{2,1,0:T(8,128)(2,1)S(1)} %get-tuple-element.108), channel_id=1, source_target_pairs={{0,20},{4,16},{8,28},{12,24},{16,4},{20,0},{24,12},{28,8},{1,21},{... | collective-permute-start | bytes 393224 | tf_op jit(solution)/shard_map/ppermute | solution.py:350
  103.9 2.7 %collective-permute-start.21 = (bf16[2,256,128]{2,1,0:T(8,128)(2,1)S(1)}, bf16[2,256,128]{2,1,0:T(8,128)(2,1)S(1)}, u32[]{:S(2)}, u32[]{:S(2)}) collective-permute-start(bf16[2,256,128]{2,1,0:T(8,128)(2,1)S(1)} %get-tuple-element.110), channel_id=1, source_target_pairs={{0,24},{4,28},{8,0},{12,4},{16,8},{20,12},{24,16},{28,20},{1,25},{... | collective-permute-start | bytes 393224 | tf_op jit(solution)/shard_map/ppermute | solution.py:350
  106.6 1.3 collective-permute-start.28
  108.0 2.8 %collective-permute-start.41 = (f32[40,128]{1,0:T(8,128)S(1)}, f32[40,128]{1,0:T(8,128)S(1)}, u32[]{:S(2)}, u32[]{:S(2)}) collective-permute-start(f32[40,128]{1,0:T(8,128)S(1)} %add_add_fusion.1), channel_id=1, source_target_pairs={{0,3},{1,0},{2,1},{3,2},{4,7},{5,4},{6,5},{7,6},{8,11},{9,8},{10,9... | collective-permute-start | bytes 61448 | tf_op jit(solution)/shard_map/ppermute | solution.py:355
  110.7 1.0 collective-permute-start.40
  112.1 1.3 collective-permute-start.39
  114.9 2.2 %collective-permute-start.23 = (bf16[2,256,128]{2,1,0:T(8,128)(2,1)S(1)}, bf16[2,256,128]{2,1,0:T(8,128)(2,1)S(1)}, u32[]{:S(2)}, u32[]{:S(2)}) collective-permute-start(bf16[2,256,128]{2,1,0:T(8,128)(2,1)S(1)} %get-tuple-element.112), channel_id=1, source_target_pairs={{0,28},{4,24},{8,4},{12,0},{16,12},{20,8},{24,20},{28,16},{1,29},{... | collective-permute-start | bytes 393224 | tf_op jit(solution)/shard_map/ppermute | solution.py:350
  117.1 2.0 %collective-permute-start.24 = (bf16[2,256,128]{2,1,0:T(8,128)(2,1)S(1)}, bf16[2,256,128]{2,1,0:T(8,128)(2,1)S(1)}, u32[]{:S(2)}, u32[]{:S(2)}) collective-permute-start(bf16[2,256,128]{2,1,0:T(8,128)(2,1)S(1)} %get-tuple-element.113), channel_id=1, source_target_pairs={{0,4},{4,0},{8,12},{12,8},{16,20},{20,16},{24,28},{28,24},{1,5},{5... | collective-permute-start | bytes 393224 | tf_op jit(solution)/shard_map/ppermute | solution.py:350
  119.1 3.2 %collective-permute-start.30 = (bf16[2,256,128]{2,1,0:T(8,128)(2,1)S(1)}, bf16[2,256,128]{2,1,0:T(8,128)(2,1)S(1)}, u32[]{:S(2)}, u32[]{:S(2)}) collective-permute-start(bf16[2,256,128]{2,1,0:T(8,128)(2,1)S(1)} %get-tuple-element.135), channel_id=1, source_target_pairs={{0,20},{4,16},{8,28},{12,24},{16,4},{20,0},{24,12},{28,8},{1,21},{... | collective-permute-start | bytes 393224 | tf_op jit(solution)/shard_map/ppermute | solution.py:350
  123.3 1.0 collective-permute-start.46
  124.3 8.8 %collective-permute-start.45 = (f32[40,128]{1,0:T(8,128)S(1)}, f32[40,128]{1,0:T(8,128)S(1)}, u32[]{:S(2)}, u32[]{:S(2)}) collective-permute-start(f32[40,128]{1,0:T(8,128)S(1)} %add_add_fusion.refs_0_), channel_id=1, source_target_pairs={{0,24},{4,28},{8,0},{12,4},{16,8},{20,12},{24,16},{28,20},{1,25},{... | collective-permute-start | bytes 61448 | tf_op jit(solution)/shard_map/ppermute | solution.py:350
  134.0 3.8 %collective-permute-start.42 = (f32[40,128]{1,0:T(8,128)S(1)}, f32[40,128]{1,0:T(8,128)S(1)}, u32[]{:S(2)}, u32[]{:S(2)}) collective-permute-start(f32[40,128]{1,0:T(8,128)S(1)} %add_add_fusion.refs_0_), channel_id=1, source_target_pairs={{0,16},{4,20},{8,24},{12,28},{16,0},{20,4},{24,8},{28,12},{1,17},{... | collective-permute-start | bytes 61448 | tf_op jit(solution)/shard_map/ppermute | solution.py:350
  137.9 2.6 %collective-permute-start.32 = (bf16[2,256,128]{2,1,0:T(8,128)(2,1)S(1)}, bf16[2,256,128]{2,1,0:T(8,128)(2,1)S(1)}, u32[]{:S(2)}, u32[]{:S(2)}) collective-permute-start(bf16[2,256,128]{2,1,0:T(8,128)(2,1)S(1)} %get-tuple-element.137), channel_id=1, source_target_pairs={{0,24},{4,28},{8,0},{12,4},{16,8},{20,12},{24,16},{28,20},{1,25},{... | collective-permute-start | bytes 393224 | tf_op jit(solution)/shard_map/ppermute | solution.py:350
  140.5 1.5 %collective-permute-start.33 = (bf16[2,256,128]{2,1,0:T(8,128)(2,1)S(1)}, bf16[2,256,128]{2,1,0:T(8,128)(2,1)S(1)}, u32[]{:S(2)}, u32[]{:S(2)}) collective-permute-start(bf16[2,256,128]{2,1,0:T(8,128)(2,1)S(1)} %get-tuple-element.138), channel_id=1, source_target_pairs={{0,12},{4,8},{8,20},{12,16},{16,28},{20,24},{24,4},{28,0},{1,13},{... | collective-permute-start | bytes 393224 | tf_op jit(solution)/shard_map/ppermute | solution.py:350
  142.0 1.4 collective-permute-start.34
  143.4 1.1 collective-permute-start.35
  144.6 1.8 %shard_map.113 = (bf16[1,256,1024]{2,1,0:T(8,128)(2,1)}, bf16[1,256,1024]{2,1,0:T(8,128)(2,1)}) custom-call(s32[3]{0:T(128)S(1)} %pad_add_fusion.pos_ref, bf16[2,256,128]{2,1,0:T(8,128)(2,1)S(1)} %get-tuple-element.106.refs_0_, bf16[2,256,128]{2,1,0:T(8,128)(2,1)S(1)} %collective-permute-done.18.refs_1_, ...), custom_call_target="tpu_custom_call" | custom-call | tf_op jit(solution)/shard_map/pallas_call | solution.py:379
  146.4 1.2 shard_map.117
  147.7 1.8 %shard_map.116 = (bf16[1,256,1024]{2,1,0:T(8,128)(2,1)}, bf16[1,256,1024]{2,1,0:T(8,128)(2,1)}) custom-call(s32[3]{0:T(128)S(1)} %pad_add_fusion.pos_ref, bf16[2,256,128]{2,1,0:T(8,128)(2,1)S(1)} %get-tuple-element.133.refs_0_, bf16[2,256,128]{2,1,0:T(8,128)(2,1)S(1)} %collective-permute-done.29.refs_1_, ...), custom_call_target="tpu_custom_call" | custom-call | tf_op jit(solution)/shard_map/pallas_call | solution.py:379
  (75 shorter events, 7.4 us)
Async XLA Ops:
  3.7 7.0 %collective-permute-start = (bf16[2,256,128]{2,1,0:T(8,128)(2,1)S(1)}, bf16[2,256,128]{2,1,0:T(8,128)(2,1)S(1)}, u32[]{:S(2)}, u32[]{:S(2)}) collective-permute-start(bf16[2,256,128]{2,1,0:T(8,128)(2,1)S(1)} %get-tuple-element.76), channel_id=1, source_target_pairs={{0,4},{4,0},{8,12},{12,8},{16,20},{20,16},{24,28},{28,24},{1,5},{5... | collective-permute-start | bytes 393224 | tf_op jit(solution)/shard_map/ppermute | solution.py:350
  5.1 7.0 %collective-permute-start.1 = (bf16[2,256,128]{2,1,0:T(8,128)(2,1)S(1)}, bf16[2,256,128]{2,1,0:T(8,128)(2,1)S(1)}, u32[]{:S(2)}, u32[]{:S(2)}) collective-permute-start(bf16[2,256,128]{2,1,0:T(8,128)(2,1)S(1)} %get-tuple-element.77), channel_id=1, source_target_pairs={{0,28},{4,24},{8,4},{12,0},{16,12},{20,8},{24,20},{28,16},{1,29},{... | collective-permute-start | bytes 393224 | tf_op jit(solution)/shard_map/ppermute | solution.py:350
  7.7 7.1 %collective-permute-start.2 = (bf16[2,256,128]{2,1,0:T(8,128)(2,1)S(1)}, bf16[2,256,128]{2,1,0:T(8,128)(2,1)S(1)}, u32[]{:S(2)}, u32[]{:S(2)}) collective-permute-start(bf16[2,256,128]{2,1,0:T(8,128)(2,1)S(1)} %get-tuple-element.78), channel_id=1, source_target_pairs={{0,12},{4,8},{8,20},{12,16},{16,28},{20,24},{24,4},{28,0},{1,13},{... | collective-permute-start | bytes 393224 | tf_op jit(solution)/shard_map/ppermute | solution.py:350
  7.7 7.1 %collective-permute-start.3 = (bf16[2,256,128]{2,1,0:T(8,128)(2,1)S(1)}, bf16[2,256,128]{2,1,0:T(8,128)(2,1)S(1)}, u32[]{:S(2)}, u32[]{:S(2)}) collective-permute-start(bf16[2,256,128]{2,1,0:T(8,128)(2,1)S(1)} %get-tuple-element.79), channel_id=1, source_target_pairs={{0,24},{4,28},{8,0},{12,4},{16,8},{20,12},{24,16},{28,20},{1,25},{... | collective-permute-start | bytes 393224 | tf_op jit(solution)/shard_map/ppermute | solution.py:350
  10.7 11.8 %collective-permute-start.4 = (bf16[2,256,128]{2,1,0:T(8,128)(2,1)S(1)}, bf16[2,256,128]{2,1,0:T(8,128)(2,1)S(1)}, u32[]{:S(2)}, u32[]{:S(2)}) collective-permute-start(bf16[2,256,128]{2,1,0:T(8,128)(2,1)S(1)} %get-tuple-element.80), channel_id=1, source_target_pairs={{0,8},{4,12},{8,16},{12,20},{16,24},{20,28},{24,0},{28,4},{1,9},{5... | collective-permute-start | bytes 393224 | tf_op jit(solution)/shard_map/ppermute | solution.py:350
  10.7 11.8 %collective-permute-start.5 = (bf16[2,256,128]{2,1,0:T(8,128)(2,1)S(1)}, bf16[2,256,128]{2,1,0:T(8,128)(2,1)S(1)}, u32[]{:S(2)}, u32[]{:S(2)}) collective-permute-start(bf16[2,256,128]{2,1,0:T(8,128)(2,1)S(1)} %get-tuple-element.81), channel_id=1, source_target_pairs={{0,20},{4,16},{8,28},{12,24},{16,4},{20,0},{24,12},{28,8},{1,21},{... | collective-permute-start | bytes 393224 | tf_op jit(solution)/shard_map/ppermute | solution.py:350
  12.1 10.4 %collective-permute-start.6 = (bf16[2,256,128]{2,1,0:T(8,128)(2,1)S(1)}, bf16[2,256,128]{2,1,0:T(8,128)(2,1)S(1)}, u32[]{:S(2)}, u32[]{:S(2)}) collective-permute-start(bf16[2,256,128]{2,1,0:T(8,128)(2,1)S(1)} %get-tuple-element.82), channel_id=1, source_target_pairs={{0,16},{4,20},{8,24},{12,28},{16,0},{20,4},{24,8},{28,12},{1,17},{... | collective-permute-start | bytes 393224 | tf_op jit(solution)/shard_map/ppermute | solution.py:350
  22.5 4.6 %collective-permute-start.14 = (bf16[2,64,128]{2,1,0:T(8,128)(2,1)S(1)}, bf16[2,64,128]{2,1,0:T(8,128)(2,1)S(1)}, u32[]{:S(2)}, u32[]{:S(2)}) collective-permute-start(bf16[2,64,128]{2,1,0:T(8,128)(2,1)S(1)} %fusion.5), channel_id=1, source_target_pairs={{0,32},{32,64},{64,96},{1,33},{33,65},{65,97},{2,34},{34,66},{66,9... | collective-permute-start | bytes 98312 | tf_op jit(solution)/shard_map/ppermute | solution.py:406
  26.0 14.4 %collective-permute-start.7 = (bf16[2,256,128]{2,1,0:T(8,128)(2,1)S(1)}, bf16[2,256,128]{2,1,0:T(8,128)(2,1)S(1)}, u32[]{:S(2)}, u32[]{:S(2)}) collective-permute-start(bf16[2,256,128]{2,1,0:T(8,128)(2,1)S(1)} %get-tuple-element.93), channel_id=1, source_target_pairs={{0,16},{4,20},{8,24},{12,28},{16,0},{20,4},{24,8},{28,12},{1,17},{... | collective-permute-start | bytes 393224 | tf_op jit(solution)/shard_map/ppermute | solution.py:350
  28.7 24.2 %collective-permute-start.15 = (bf16[1408,128]{1,0:T(8,128)(2,1)S(1)}, bf16[1408,128]{1,0:T(8,128)(2,1)S(1)}, u32[]{:S(2)}, u32[]{:S(2)}) collective-permute-start(bf16[1408,128]{1,0:T(8,128)(2,1)S(1)} %get-tuple-element.103), channel_id=1, source_target_pairs={{0,32},{32,64},{64,96},{96,0},{1,33},{33,65},{65,97},{97,1},{2,34}... | collective-permute-start | bytes 1081352 | tf_op jit(solution)/shard_map/ppermute | solution.py:355
  30.5 22.4 %collective-permute-start.16 = (bf16[1408,128]{1,0:T(8,128)(2,1)S(1)}, bf16[1408,128]{1,0:T(8,128)(2,1)S(1)}, u32[]{:S(2)}, u32[]{:S(2)}) collective-permute-start(bf16[1408,128]{1,0:T(8,128)(2,1)S(1)} %get-tuple-element.104), channel_id=1, source_target_pairs={{0,96},{32,0},{64,32},{96,64},{1,97},{33,1},{65,33},{97,65},{2,98}... | collective-permute-start | bytes 1081352 | tf_op jit(solution)/shard_map/ppermute | solution.py:355
  32.7 7.8 %collective-permute-start.17 = (bf16[128,128]{1,0:T(8,128)(2,1)S(1)}, bf16[128,128]{1,0:T(8,128)(2,1)S(1)}, u32[]{:S(2)}, u32[]{:S(2)}) collective-permute-start(bf16[128,128]{1,0:T(8,128)(2,1)S(1)} %get-tuple-element.105), channel_id=1, source_target_pairs={{0,64},{32,96},{64,0},{96,32},{1,65},{33,97},{65,1},{97,33},{2,66}... | collective-permute-start | bytes 98312 | tf_op jit(solution)/shard_map/ppermute | solution.py:359
  33.9 9.2 %collective-permute-start.8 = (bf16[2,256,128]{2,1,0:T(8,128)(2,1)S(1)}, bf16[2,256,128]{2,1,0:T(8,128)(2,1)S(1)}, u32[]{:S(2)}, u32[]{:S(2)}) collective-permute-start(bf16[2,256,128]{2,1,0:T(8,128)(2,1)S(1)} %get-tuple-element.94), channel_id=1, source_target_pairs={{0,20},{4,16},{8,28},{12,24},{16,4},{20,0},{24,12},{28,8},{1,21},{... | collective-permute-start | bytes 393224 | tf_op jit(solution)/shard_map/ppermute | solution.py:350
  40.5 5.0 %collective-permute-start.9 = (bf16[2,256,128]{2,1,0:T(8,128)(2,1)S(1)}, bf16[2,256,128]{2,1,0:T(8,128)(2,1)S(1)}, u32[]{:S(2)}, u32[]{:S(2)}) collective-permute-start(bf16[2,256,128]{2,1,0:T(8,128)(2,1)S(1)} %get-tuple-element.95), channel_id=1, source_target_pairs={{0,8},{4,12},{8,16},{12,20},{16,24},{20,28},{24,0},{28,4},{1,9},{5... | collective-permute-start | bytes 393224 | tf_op jit(solution)/shard_map/ppermute | solution.py:350
  40.5 9.4 %collective-permute-start.10 = (bf16[2,256,128]{2,1,0:T(8,128)(2,1)S(1)}, bf16[2,256,128]{2,1,0:T(8,128)(2,1)S(1)}, u32[]{:S(2)}, u32[]{:S(2)}) collective-permute-start(bf16[2,256,128]{2,1,0:T(8,128)(2,1)S(1)} %get-tuple-element.96), channel_id=1, source_target_pairs={{0,24},{4,28},{8,0},{12,4},{16,8},{20,12},{24,16},{28,20},{1,25},{... | collective-permute-start | bytes 393224 | tf_op jit(solution)/shard_map/ppermute | solution.py:350
  43.1 8.0 %collective-permute-start.11 = (bf16[2,256,128]{2,1,0:T(8,128)(2,1)S(1)}, bf16[2,256,128]{2,1,0:T(8,128)(2,1)S(1)}, u32[]{:S(2)}, u32[]{:S(2)}) collective-permute-start(bf16[2,256,128]{2,1,0:T(8,128)(2,1)S(1)} %get-tuple-element.97), channel_id=1, source_target_pairs={{0,12},{4,8},{8,20},{12,16},{16,28},{20,24},{24,4},{28,0},{1,13},{... | collective-permute-start | bytes 393224 | tf_op jit(solution)/shard_map/ppermute | solution.py:350
  45.5 7.4 %collective-permute-start.12 = (bf16[2,256,128]{2,1,0:T(8,128)(2,1)S(1)}, bf16[2,256,128]{2,1,0:T(8,128)(2,1)S(1)}, u32[]{:S(2)}, u32[]{:S(2)}) collective-permute-start(bf16[2,256,128]{2,1,0:T(8,128)(2,1)S(1)} %get-tuple-element.98), channel_id=1, source_target_pairs={{0,28},{4,24},{8,4},{12,0},{16,12},{20,8},{24,20},{28,16},{1,29},{... | collective-permute-start | bytes 393224 | tf_op jit(solution)/shard_map/ppermute | solution.py:350
  49.9 3.0 %collective-permute-start.13 = (bf16[2,256,128]{2,1,0:T(8,128)(2,1)S(1)}, bf16[2,256,128]{2,1,0:T(8,128)(2,1)S(1)}, u32[]{:S(2)}, u32[]{:S(2)}) collective-permute-start(bf16[2,256,128]{2,1,0:T(8,128)(2,1)S(1)} %get-tuple-element.99), channel_id=1, source_target_pairs={{0,4},{4,0},{8,12},{12,8},{16,20},{20,16},{24,28},{28,24},{1,5},{5... | collective-permute-start | bytes 393224 | tf_op jit(solution)/shard_map/ppermute | solution.py:350
  80.7 10.1 %collective-permute-start.25 = (bf16[1408,128]{1,0:T(8,128)(2,1)S(1)}, bf16[1408,128]{1,0:T(8,128)(2,1)S(1)}, u32[]{:S(2)}, u32[]{:S(2)}) collective-permute-start(bf16[1408,128]{1,0:T(8,128)(2,1)S(1)} %get-tuple-element.118), channel_id=1, source_target_pairs={{0,32},{32,64},{64,96},{96,0},{1,33},{33,65},{65,97},{97,1},{2,34}... | collective-permute-start | bytes 1081352 | tf_op jit(solution)/shard_map/ppermute | solution.py:355
  81.6 9.1 %collective-permute-start.26 = (bf16[1408,128]{1,0:T(8,128)(2,1)S(1)}, bf16[1408,128]{1,0:T(8,128)(2,1)S(1)}, u32[]{:S(2)}, u32[]{:S(2)}) collective-permute-start(bf16[1408,128]{1,0:T(8,128)(2,1)S(1)} %get-tuple-element.119), channel_id=1, source_target_pairs={{0,96},{32,0},{64,32},{96,64},{1,97},{33,1},{65,33},{97,65},{2,98}... | collective-permute-start | bytes 1081352 | tf_op jit(solution)/shard_map/ppermute | solution.py:355
  83.4 6.7 %collective-permute-start.27 = (bf16[128,128]{1,0:T(8,128)(2,1)S(1)}, bf16[128,128]{1,0:T(8,128)(2,1)S(1)}, u32[]{:S(2)}, u32[]{:S(2)}) collective-permute-start(bf16[128,128]{1,0:T(8,128)(2,1)S(1)} %get-tuple-element.120), channel_id=1, source_target_pairs={{0,64},{32,96},{64,0},{96,32},{1,65},{33,97},{65,1},{97,33},{2,66}... | collective-permute-start | bytes 98312 | tf_op jit(solution)/shard_map/ppermute | solution.py:359
  93.2 9.8 %collective-permute-start.38 = (f32[40,128]{1,0:T(8,128)S(1)}, f32[40,128]{1,0:T(8,128)S(1)}, u32[]{:S(2)}, u32[]{:S(2)}) collective-permute-start(f32[40,128]{1,0:T(8,128)S(1)} %get-tuple-element.143), channel_id=1, source_target_pairs={{0,96},{32,0},{64,32},{96,64},{1,97},{33,1},{65,33},{97,65},{2,98}... | collective-permute-start | bytes 61448 | tf_op jit(solution)/shard_map/ppermute | solution.py:355
  95.7 8.2 %collective-permute-start.37 = (f32[40,128]{1,0:T(8,128)S(1)}, f32[40,128]{1,0:T(8,128)S(1)}, u32[]{:S(2)}, u32[]{:S(2)}) collective-permute-start(f32[40,128]{1,0:T(8,128)S(1)} %get-tuple-element.143), channel_id=1, source_target_pairs={{0,64},{32,96},{64,0},{96,32},{1,65},{33,97},{65,1},{97,33},{2,66}... | collective-permute-start | bytes 61448 | tf_op jit(solution)/shard_map/ppermute | solution.py:355
  95.7 10.9 %collective-permute-start.36 = (f32[40,128]{1,0:T(8,128)S(1)}, f32[40,128]{1,0:T(8,128)S(1)}, u32[]{:S(2)}, u32[]{:S(2)}) collective-permute-start(f32[40,128]{1,0:T(8,128)S(1)} %get-tuple-element.143), channel_id=1, source_target_pairs={{0,32},{32,64},{64,96},{96,0},{1,33},{33,65},{65,97},{97,1},{2,34}... | collective-permute-start | bytes 61448 | tf_op jit(solution)/shard_map/ppermute | solution.py:355
  96.4 11.6 %collective-permute-start.18 = (bf16[2,256,128]{2,1,0:T(8,128)(2,1)S(1)}, bf16[2,256,128]{2,1,0:T(8,128)(2,1)S(1)}, u32[]{:S(2)}, u32[]{:S(2)}) collective-permute-start(bf16[2,256,128]{2,1,0:T(8,128)(2,1)S(1)} %get-tuple-element.107), channel_id=1, source_target_pairs={{0,16},{4,20},{8,24},{12,28},{16,0},{20,4},{24,8},{28,12},{1,17},{... | collective-permute-start | bytes 393224 | tf_op jit(solution)/shard_map/ppermute | solution.py:350
  99.5 11.3 %collective-permute-start.19 = (bf16[2,256,128]{2,1,0:T(8,128)(2,1)S(1)}, bf16[2,256,128]{2,1,0:T(8,128)(2,1)S(1)}, u32[]{:S(2)}, u32[]{:S(2)}) collective-permute-start(bf16[2,256,128]{2,1,0:T(8,128)(2,1)S(1)} %get-tuple-element.108), channel_id=1, source_target_pairs={{0,20},{4,16},{8,28},{12,24},{16,4},{20,0},{24,12},{28,8},{1,21},{... | collective-permute-start | bytes 393224 | tf_op jit(solution)/shard_map/ppermute | solution.py:350
  103.1 11.0 %collective-permute-start.20 = (bf16[2,256,128]{2,1,0:T(8,128)(2,1)S(1)}, bf16[2,256,128]{2,1,0:T(8,128)(2,1)S(1)}, u32[]{:S(2)}, u32[]{:S(2)}) collective-permute-start(bf16[2,256,128]{2,1,0:T(8,128)(2,1)S(1)} %get-tuple-element.109), channel_id=1, source_target_pairs={{0,8},{4,12},{8,16},{12,20},{16,24},{20,28},{24,0},{28,4},{1,9},{5... | collective-permute-start | bytes 393224 | tf_op jit(solution)/shard_map/ppermute | solution.py:350
  103.9 11.0 %collective-permute-start.21 = (bf16[2,256,128]{2,1,0:T(8,128)(2,1)S(1)}, bf16[2,256,128]{2,1,0:T(8,128)(2,1)S(1)}, u32[]{:S(2)}, u32[]{:S(2)}) collective-permute-start(bf16[2,256,128]{2,1,0:T(8,128)(2,1)S(1)} %get-tuple-element.110), channel_id=1, source_target_pairs={{0,24},{4,28},{8,0},{12,4},{16,8},{20,12},{24,16},{28,20},{1,25},{... | collective-permute-start | bytes 393224 | tf_op jit(solution)/shard_map/ppermute | solution.py:350
  106.6 5.5 %collective-permute-start.28 = (bf16[2,64,128]{2,1,0:T(8,128)(2,1)S(1)}, bf16[2,64,128]{2,1,0:T(8,128)(2,1)S(1)}, u32[]{:S(2)}, u32[]{:S(2)}) collective-permute-start(bf16[2,64,128]{2,1,0:T(8,128)(2,1)S(1)} %get-tuple-element.132), channel_id=1, source_target_pairs={{32,0},{64,32},{96,64},{33,1},{65,33},{97,65},{34,2},{66,34},{98,6... | collective-permute-start | bytes 98312 | tf_op jit(solution)/shard_map/ppermute | solution.py:440
  108.0 9.1 %collective-permute-start.41 = (f32[40,128]{1,0:T(8,128)S(1)}, f32[40,128]{1,0:T(8,128)S(1)}, u32[]{:S(2)}, u32[]{:S(2)}) collective-permute-start(f32[40,128]{1,0:T(8,128)S(1)} %add_add_fusion.1), channel_id=1, source_target_pairs={{0,3},{1,0},{2,1},{3,2},{4,7},{5,4},{6,5},{7,6},{8,11},{9,8},{10,9... | collective-permute-start | bytes 61448 | tf_op jit(solution)/shard_map/ppermute | solution.py:355
  110.7 8.3 %collective-permute-start.40 = (f32[40,128]{1,0:T(8,128)S(1)}, f32[40,128]{1,0:T(8,128)S(1)}, u32[]{:S(2)}, u32[]{:S(2)}) collective-permute-start(f32[40,128]{1,0:T(8,128)S(1)} %add_add_fusion.1), channel_id=1, source_target_pairs={{0,2},{1,3},{2,0},{3,1},{4,6},{5,7},{6,4},{7,5},{8,10},{9,11},{10,... | collective-permute-start | bytes 61448 | tf_op jit(solution)/shard_map/ppermute | solution.py:355
  112.1 6.9 %collective-permute-start.39 = (f32[40,128]{1,0:T(8,128)S(1)}, f32[40,128]{1,0:T(8,128)S(1)}, u32[]{:S(2)}, u32[]{:S(2)}) collective-permute-start(f32[40,128]{1,0:T(8,128)S(1)} %add_add_fusion.1), channel_id=1, source_target_pairs={{0,1},{1,2},{2,3},{3,0},{4,5},{5,6},{6,7},{7,4},{8,9},{9,10},{10,1... | collective-permute-start | bytes 61448 | tf_op jit(solution)/shard_map/ppermute | solution.py:355
  114.1 8.2 %collective-permute-start.22 = (bf16[2,256,128]{2,1,0:T(8,128)(2,1)S(1)}, bf16[2,256,128]{2,1,0:T(8,128)(2,1)S(1)}, u32[]{:S(2)}, u32[]{:S(2)}) collective-permute-start(bf16[2,256,128]{2,1,0:T(8,128)(2,1)S(1)} %get-tuple-element.111), channel_id=1, source_target_pairs={{0,12},{4,8},{8,20},{12,16},{16,28},{20,24},{24,4},{28,0},{1,13},{... | collective-permute-start | bytes 393224 | tf_op jit(solution)/shard_map/ppermute | solution.py:350
  114.9 7.7 %collective-permute-start.23 = (bf16[2,256,128]{2,1,0:T(8,128)(2,1)S(1)}, bf16[2,256,128]{2,1,0:T(8,128)(2,1)S(1)}, u32[]{:S(2)}, u32[]{:S(2)}) collective-permute-start(bf16[2,256,128]{2,1,0:T(8,128)(2,1)S(1)} %get-tuple-element.112), channel_id=1, source_target_pairs={{0,28},{4,24},{8,4},{12,0},{16,12},{20,8},{24,20},{28,16},{1,29},{... | collective-permute-start | bytes 393224 | tf_op jit(solution)/shard_map/ppermute | solution.py:350
  117.1 6.2 %collective-permute-start.24 = (bf16[2,256,128]{2,1,0:T(8,128)(2,1)S(1)}, bf16[2,256,128]{2,1,0:T(8,128)(2,1)S(1)}, u32[]{:S(2)}, u32[]{:S(2)}) collective-permute-start(bf16[2,256,128]{2,1,0:T(8,128)(2,1)S(1)} %get-tuple-element.113), channel_id=1, source_target_pairs={{0,4},{4,0},{8,12},{12,8},{16,20},{20,16},{24,28},{28,24},{1,5},{5... | collective-permute-start | bytes 393224 | tf_op jit(solution)/shard_map/ppermute | solution.py:350
  119.1 22.9 %collective-permute-start.29 = (bf16[2,256,128]{2,1,0:T(8,128)(2,1)S(1)}, bf16[2,256,128]{2,1,0:T(8,128)(2,1)S(1)}, u32[]{:S(2)}, u32[]{:S(2)}) collective-permute-start(bf16[2,256,128]{2,1,0:T(8,128)(2,1)S(1)} %get-tuple-element.134), channel_id=1, source_target_pairs={{0,16},{4,20},{8,24},{12,28},{16,0},{20,4},{24,8},{28,12},{1,17},{... | collective-permute-start | bytes 393224 | tf_op jit(solution)/shard_map/ppermute | solution.py:350
  119.1 24.4 %collective-permute-start.30 = (bf16[2,256,128]{2,1,0:T(8,128)(2,1)S(1)}, bf16[2,256,128]{2,1,0:T(8,128)(2,1)S(1)}, u32[]{:S(2)}, u32[]{:S(2)}) collective-permute-start(bf16[2,256,128]{2,1,0:T(8,128)(2,1)S(1)} %get-tuple-element.135), channel_id=1, source_target_pairs={{0,20},{4,16},{8,28},{12,24},{16,4},{20,0},{24,12},{28,8},{1,21},{... | collective-permute-start | bytes 393224 | tf_op jit(solution)/shard_map/ppermute | solution.py:350
  122.5 10.5 %collective-permute-start.47 = (f32[40,128]{1,0:T(8,128)S(1)}, f32[40,128]{1,0:T(8,128)S(1)}, u32[]{:S(2)}, u32[]{:S(2)}) collective-permute-start(f32[40,128]{1,0:T(8,128)S(1)} %add_add_fusion.refs_0_), channel_id=1, source_target_pairs={{0,28},{4,24},{8,4},{12,0},{16,12},{20,8},{24,20},{28,16},{1,29},{... | collective-permute-start | bytes 61448 | tf_op jit(solution)/shard_map/ppermute | solution.py:350
  123.3 9.8 %collective-permute-start.46 = (f32[40,128]{1,0:T(8,128)S(1)}, f32[40,128]{1,0:T(8,128)S(1)}, u32[]{:S(2)}, u32[]{:S(2)}) collective-permute-start(f32[40,128]{1,0:T(8,128)S(1)} %add_add_fusion.refs_0_), channel_id=1, source_target_pairs={{0,12},{4,8},{8,20},{12,16},{16,28},{20,24},{24,4},{28,0},{1,13},{... | collective-permute-start | bytes 61448 | tf_op jit(solution)/shard_map/ppermute | solution.py:350
  124.3 9.7 %collective-permute-start.45 = (f32[40,128]{1,0:T(8,128)S(1)}, f32[40,128]{1,0:T(8,128)S(1)}, u32[]{:S(2)}, u32[]{:S(2)}) collective-permute-start(f32[40,128]{1,0:T(8,128)S(1)} %add_add_fusion.refs_0_), channel_id=1, source_target_pairs={{0,24},{4,28},{8,0},{12,4},{16,8},{20,12},{24,16},{28,20},{1,25},{... | collective-permute-start | bytes 61448 | tf_op jit(solution)/shard_map/ppermute | solution.py:350
  133.1 4.7 %collective-permute-start.44 = (f32[40,128]{1,0:T(8,128)S(1)}, f32[40,128]{1,0:T(8,128)S(1)}, u32[]{:S(2)}, u32[]{:S(2)}) collective-permute-start(f32[40,128]{1,0:T(8,128)S(1)} %add_add_fusion.refs_0_), channel_id=1, source_target_pairs={{0,8},{4,12},{8,16},{12,20},{16,24},{20,28},{24,0},{28,4},{1,9},{5... | collective-permute-start | bytes 61448 | tf_op jit(solution)/shard_map/ppermute | solution.py:350
  133.1 4.8 %collective-permute-start.43 = (f32[40,128]{1,0:T(8,128)S(1)}, f32[40,128]{1,0:T(8,128)S(1)}, u32[]{:S(2)}, u32[]{:S(2)}) collective-permute-start(f32[40,128]{1,0:T(8,128)S(1)} %add_add_fusion.refs_0_), channel_id=1, source_target_pairs={{0,20},{4,16},{8,28},{12,24},{16,4},{20,0},{24,12},{28,8},{1,21},{... | collective-permute-start | bytes 61448 | tf_op jit(solution)/shard_map/ppermute | solution.py:350
  134.0 6.5 %collective-permute-start.42 = (f32[40,128]{1,0:T(8,128)S(1)}, f32[40,128]{1,0:T(8,128)S(1)}, u32[]{:S(2)}, u32[]{:S(2)}) collective-permute-start(f32[40,128]{1,0:T(8,128)S(1)} %add_add_fusion.refs_0_), channel_id=1, source_target_pairs={{0,16},{4,20},{8,24},{12,28},{16,0},{20,4},{24,8},{28,12},{1,17},{... | collective-permute-start | bytes 61448 | tf_op jit(solution)/shard_map/ppermute | solution.py:350
  137.8 9.9 %collective-permute-start.31 = (bf16[2,256,128]{2,1,0:T(8,128)(2,1)S(1)}, bf16[2,256,128]{2,1,0:T(8,128)(2,1)S(1)}, u32[]{:S(2)}, u32[]{:S(2)}) collective-permute-start(bf16[2,256,128]{2,1,0:T(8,128)(2,1)S(1)} %get-tuple-element.136), channel_id=1, source_target_pairs={{0,8},{4,12},{8,16},{12,20},{16,24},{20,28},{24,0},{28,4},{1,9},{5... | collective-permute-start | bytes 393224 | tf_op jit(solution)/shard_map/ppermute | solution.py:350
  137.9 9.8 %collective-permute-start.32 = (bf16[2,256,128]{2,1,0:T(8,128)(2,1)S(1)}, bf16[2,256,128]{2,1,0:T(8,128)(2,1)S(1)}, u32[]{:S(2)}, u32[]{:S(2)}) collective-permute-start(bf16[2,256,128]{2,1,0:T(8,128)(2,1)S(1)} %get-tuple-element.137), channel_id=1, source_target_pairs={{0,24},{4,28},{8,0},{12,4},{16,8},{20,12},{24,16},{28,20},{1,25},{... | collective-permute-start | bytes 393224 | tf_op jit(solution)/shard_map/ppermute | solution.py:350
  140.5 7.2 %collective-permute-start.33 = (bf16[2,256,128]{2,1,0:T(8,128)(2,1)S(1)}, bf16[2,256,128]{2,1,0:T(8,128)(2,1)S(1)}, u32[]{:S(2)}, u32[]{:S(2)}) collective-permute-start(bf16[2,256,128]{2,1,0:T(8,128)(2,1)S(1)} %get-tuple-element.138), channel_id=1, source_target_pairs={{0,12},{4,8},{8,20},{12,16},{16,28},{20,24},{24,4},{28,0},{1,13},{... | collective-permute-start | bytes 393224 | tf_op jit(solution)/shard_map/ppermute | solution.py:350
  142.0 5.7 %collective-permute-start.34 = (bf16[2,256,128]{2,1,0:T(8,128)(2,1)S(1)}, bf16[2,256,128]{2,1,0:T(8,128)(2,1)S(1)}, u32[]{:S(2)}, u32[]{:S(2)}) collective-permute-start(bf16[2,256,128]{2,1,0:T(8,128)(2,1)S(1)} %get-tuple-element.139), channel_id=1, source_target_pairs={{0,28},{4,24},{8,4},{12,0},{16,12},{20,8},{24,20},{28,16},{1,29},{... | collective-permute-start | bytes 393224 | tf_op jit(solution)/shard_map/ppermute | solution.py:350
  143.4 4.2 %collective-permute-start.35 = (bf16[2,256,128]{2,1,0:T(8,128)(2,1)S(1)}, bf16[2,256,128]{2,1,0:T(8,128)(2,1)S(1)}, u32[]{:S(2)}, u32[]{:S(2)}) collective-permute-start(bf16[2,256,128]{2,1,0:T(8,128)(2,1)S(1)} %get-tuple-element.140), channel_id=1, source_target_pairs={{0,4},{4,0},{8,12},{12,8},{16,20},{20,16},{24,28},{28,24},{1,5},{5... | collective-permute-start | bytes 393224 | tf_op jit(solution)/shard_map/ppermute | solution.py:350
  (7 other events, 74.7 us)
